TPU v7x, 128 devices: a whole 4x4x4 slice. The times are simulated.
128 devices in a mesh: dp: 16 (over z_lo, x, core), ctx: 8 (over y, z_hi).
Axes of the slice: x: 4, y: 4, z: 4 (z_hi: 2, z_lo: 2; z = z_hi * 2 + z_lo), core: 2. Of those that a mesh axis runs over, the one named last changes fastest.
Arguments:
- inputs: bfloat16 [16, 2048, 4096], P('dp', 'ctx'), may hold values from -0.4375 to 0.4375
- queries: bfloat16 [16, 2048, 512], P('dp', 'ctx'), may hold values from -6 to 6
- keys: bfloat16 [16, 2048, 512], P('dp', 'ctx'), may hold values from -6 to 6
- values: bfloat16 [16, 2048, 512], P('dp', 'ctx'), may hold values from -6 to 6
- attn_out: bfloat16 [16, 2048, 512], P('dp', 'ctx'), may hold values from -6 to 6
- grad_out: bfloat16 [16, 2048, 512], P('dp', 'ctx'), may hold values from -96 to 96
- lse_shift: float32 [16, 4, 2048], P('dp', None, 'ctx'), may hold values from -1 to 1
- labels: int32 [16, 16], P('dp'), may hold values from 0 to 2, as said below
- layout: int32 [16, 16], P('dp'), may hold values from 0 to 15, each once within a row
Outputs:
- grad_q: bfloat16 [16, 2048, 512], P('dp', 'ctx')
- grad_k: bfloat16 [16, 2048, 512], P('dp', 'ctx')
- grad_v: bfloat16 [16, 2048, 512], P('dp', 'ctx')
- grad_w: float32 [4096, 1536], P(('dp', 'ctx'))
Inputs may be any that keep to these rules, and one draw needn't show every extreme that they name: `labels`: in a pair's natural tile order the prompt (label 0) comes first and covers 8 to 12 tiles, then the chosen response (label 1), then the rejected response (label 2), each response one tile or more. `layout`: each pair's row names every tile once.
All inputs are finite; a program needn't handle non-finite values.
Results may differ from a plain program's by a relative error of at most 0.0058.
Values may be sent and summed in bfloat16 or wider, within the bound.
A program may use at most 128 MiB of HBM per device.

v0:
```python
import math

import jax
import jax.numpy as jnp
from jax import lax
from jax.sharding import PartitionSpec as P

HEAD_DIM = 128
HEADS = 4
TILE = 128


def shifted(array, axis, by):
    peers = lax.axis_size(axis)
    return lax.ppermute(array, axis, [(i, (i + by) % peers) for i in range(peers)])


def stored_labels(label_row, layout_row):
    tile_ids = jnp.arange(label_row.shape[0], dtype=jnp.int32)
    matches = (layout_row[:, None] == tile_ids[None, :]).astype(jnp.int32)
    return jnp.sum(matches * label_row[None, :], axis=1)


def log_norms(tile_labels, own_labels, shift_rows):
    label_kinds = jnp.arange(3, dtype=jnp.int32)
    per_kind = (
        jnp.sum((tile_labels[:, None] == label_kinds[None, :]).astype(jnp.int32), axis=0) * TILE
    )
    own_match = (own_labels[:, None] == label_kinds[None, :]).astype(jnp.int32)
    own_count = jnp.sum(own_match * per_kind[None, :], axis=1)
    visible = per_kind[0] + jnp.where(own_labels != 0, own_count, 0)
    return jnp.log(visible.astype(jnp.float32))[None, :] + shift_rows


def split_heads(matrix_rows):
    return matrix_rows.reshape(matrix_rows.shape[0], HEADS, HEAD_DIM)


def block_core(
    query_rows, grad_rows, log_norm, deltas, query_labels, key_rows, value_rows, key_labels
):
    scaling = 1.0 / math.sqrt(HEAD_DIM)
    scores = (
        jnp.einsum(
            "qhd,khd->hqk",
            split_heads(query_rows),
            split_heads(key_rows),
            preferred_element_type=jnp.float32,
        )
        * scaling
    )
    allowed = (key_labels[None, :] == 0) | (query_labels[:, None] == key_labels[None, :])
    weights = jnp.where(allowed[None], jnp.exp(scores - log_norm[:, :, None]), 0.0)
    through = jnp.einsum(
        "qhd,khd->hqk",
        split_heads(grad_rows),
        split_heads(value_rows),
        preferred_element_type=jnp.float32,
    )
    dscore = (weights * (through - deltas[:, :, None]) * scaling).astype(jnp.bfloat16)
    return (weights.astype(jnp.bfloat16), dscore)


def row_part(matrix, key_rows):
    result = jnp.einsum(
        "hqk,khd->qhd", matrix, split_heads(key_rows), preferred_element_type=jnp.float32
    )
    return result.reshape(matrix.shape[1], HEADS * HEAD_DIM)


def column_part(matrix, query_rows):
    result = jnp.einsum(
        "hqk,qhd->khd", matrix, split_heads(query_rows), preferred_element_type=jnp.float32
    )
    return result.reshape(matrix.shape[2], HEADS * HEAD_DIM)


def per_device(inputs, queries, keys, values, attn_out, grad_out, lse_shift, labels, layout):
    feature_rows = inputs[0]
    query_rows = queries[0]
    key_rows = keys[0]
    value_rows = values[0]
    grad_rows = grad_out[0]
    members = lax.axis_size("ctx")
    position = lax.axis_index("ctx")
    rows_dev = query_rows.shape[0]
    tile_labels = stored_labels(labels[0], layout[0])
    token_labels = jnp.repeat(tile_labels, TILE, total_repeat_length=members * rows_dev)
    own_labels = lax.dynamic_slice_in_dim(token_labels, position * rows_dev, rows_dev)
    log_norm = log_norms(tile_labels, own_labels, lse_shift[0])
    deltas = jnp.einsum(
        "thd,thd->ht",
        split_heads(grad_rows),
        split_heads(attn_out[0]),
        preferred_element_type=jnp.float32,
    )
    zero_rows = jnp.zeros(query_rows.shape, jnp.float32)
    grad_q_sum = zero_rows
    moving_keys, moving_values = (key_rows, value_rows)
    moving_gk, moving_gv = (zero_rows, zero_rows)
    for offset in range(members):
        weights, dscore = block_core(
            query_rows,
            grad_rows,
            log_norm,
            deltas,
            own_labels,
            moving_keys,
            moving_values,
            lax.dynamic_slice_in_dim(
                token_labels, (position - offset) % members * rows_dev, rows_dev
            ),
        )
        grad_q_sum = grad_q_sum + row_part(dscore, moving_keys)
        moving_gk = moving_gk + column_part(dscore, query_rows)
        moving_gv = moving_gv + column_part(weights, grad_rows)
        if offset < members - 1:
            moving_keys, moving_values = shifted((moving_keys, moving_values), "ctx", 1)
        moving_gk, moving_gv = shifted((moving_gk, moving_gv), "ctx", 1)
    grad_k_sum, grad_v_sum = (moving_gk, moving_gv)
    grad_q = grad_q_sum.astype(jnp.bfloat16)
    grad_k = grad_k_sum.astype(jnp.bfloat16)
    grad_v = grad_v_sum.astype(jnp.bfloat16)
    stacked = jnp.concatenate([grad_q, grad_k, grad_v], axis=1)
    grad_w = lax.psum_scatter(
        lax.dot_general(
            feature_rows, stacked, (((0,), (0,)), ((), ())), preferred_element_type=jnp.float32
        ),
        ("dp", "ctx"),
        scatter_dimension=0,
        tiled=True,
    )
    return (grad_q[None], grad_k[None], grad_v[None], grad_w)


def solution(mesh):
    in_specs = (
        P("dp", "ctx", None),
        P("dp", "ctx", None),
        P("dp", "ctx", None),
        P("dp", "ctx", None),
        P("dp", "ctx", None),
        P("dp", "ctx", None),
        P("dp", None, "ctx"),
        P("dp", None),
        P("dp", None),
    )
    out_specs = (
        P("dp", "ctx", None),
        P("dp", "ctx", None),
        P("dp", "ctx", None),
        P(("dp", "ctx"), None),
    )
    return jax.shard_map(
        per_device, mesh=mesh, in_specs=in_specs, out_specs=out_specs, check_vma=False
    )
```

profile of v0, /device:TPU:0, one launch (start us, length us, event | category | flops | bytes accessed | tf_op | source)
XLA Modules:
  0.0 1097.9 jit_solution(12287880859781570588)
XLA Ops:
  7.2 2.0 copy.222
  9.2 4.0 collective-permute-start.1
  16.7 1.7 reshape_squeeze.13
  19.0 4.4 compare_select_fusion.1
  27.0 6.4 select_select_fusion
  39.6 2.0 copy.250
  41.7 3.9 collective-permute-start.14
  45.5 2.3 fusion.70
  47.8 2.0 copy.266
  55.3 2.1 copy.268
  58.4 2.0 copy.252
  60.5 3.9 collective-permute-start.3
  64.7 2.2 convolution_add_fusion.6
  66.9 14.1 %collective-permute-done.2 = bf16[256,512]{0,1:T(8,128)(2,1)S(1)} collective-permute-done((bf16[256,512]{0,1:T(8,128)(2,1)}, bf16[256,512]{0,1:T(8,128)(2,1)S(1)}, u32[]{:S(2)}, u32[]{:S(2)}) %collective-permute-start.2) | collective-permute-done | bytes 262176 | tf_op jit(solution)/shard_map/ppermute | solution.py:15
  87.3 2.0 copy.254
  89.3 2.1 add.300
  91.5 1.8 collective-permute-start.15
  93.2 2.1 add.307
  96.9 3.0 collective-permute-start.5
  102.3 27.7 %collective-permute-done.4 = bf16[256,512]{0,1:T(8,128)(2,1)S(1)} collective-permute-done((bf16[256,512]{0,1:T(8,128)(2,1)S(1)}, bf16[256,512]{0,1:T(8,128)(2,1)S(1)}, u32[]{:S(2)}, u32[]{:S(2)}) %collective-permute-start.4) | collective-permute-done | bytes 262176 | tf_op jit(solution)/shard_map/ppermute | solution.py:15
  132.8 2.1 copy.272
  135.9 2.0 copy.256
  137.9 2.1 collective-permute-start.6
  140.0 2.2 convolution_add_fusion.4
  142.3 10.8 collective-permute-done.6
  159.3 2.0 copy.258
  161.4 2.1 add.301
  163.5 2.1 add.308
  167.7 3.4 collective-permute-start.8
  172.1 28.3 %collective-permute-done.8 = bf16[256,512]{0,1:T(8,128)(2,1)S(1)} collective-permute-done((bf16[256,512]{0,1:T(8,128)(2,1)S(1)}, bf16[256,512]{0,1:T(8,128)(2,1)S(1)}, u32[]{:S(2)}, u32[]{:S(2)}) %collective-permute-start.8) | collective-permute-done | bytes 262176 | tf_op jit(solution)/shard_map/ppermute | solution.py:15
  203.2 2.0 copy.276
  206.3 2.0 copy.260
  208.4 2.3 convolution_add_fusion.2
  210.7 1.9 add.302
  212.7 1.9 add.309
  214.6 4.2 collective-permute-start.25
  218.8 8.2 collective-permute-done.10
  229.7 1.7 fusion.42
  231.4 6.9 collective-permute-done.17
  238.3 2.1 add.303
  240.4 9.2 collective-permute-done.25
  249.5 1.9 add.310
  252.5 2.0 copy.262
  254.9 2.2 convolution_add_fusion.1
  257.0 3.7 collective-permute-done.18
  260.8 1.9 add.304
  262.7 9.3 collective-permute-done.26
  272.0 1.9 add.311
  273.9 9.2 collective-permute-done.12
  285.6 2.1 copy.280
  287.7 6.8 collective-permute-done.19
  294.5 2.1 add.305
  296.6 9.2 collective-permute-done.27
  305.7 1.9 add.312
  310.0 2.1 copy.264
  312.1 4.9 collective-permute-done.20
  317.0 2.0 add.306
  318.9 7.2 collective-permute-done.28
  326.1 1.8 add.313
  329.5 2.0 collective-permute-done.21
  331.5 6.6 collective-permute-done.29
  338.1 10.1 convolution_bitcast_fusion
  348.2 24.7 %copy.306 = f32[4096,1536]{1,0:T(8,128)} copy(f32[4096,1536]{0,1:T(8,128)} %convolution_bitcast_fusion) | data formatting | bytes 50331648
  373.8 715.8 %reduce-scatter.4.cloned.1.call-done = f32[32,1536]{1,0:T(8,128)} async-done(((f32[4096,1536]{1,0:T(8,128)}), f32[32,1536]{1,0:T(8,128)}) %reduce-scatter.4.cloned.1.call-update) | async-done | bytes 196624
  (147 shorter events, 60.6 us)
Async XLA Ops:
  7.2 330.9 %copy-start = (bf16[1,256,4096]{2,1,0:T(8,128)(2,1)S(1)}, bf16[1,256,4096]{2,1,0:T(8,128)(2,1)}, u32[]{:S(2)}) copy-start(bf16[1,256,4096]{2,1,0:T(8,128)(2,1)} %param.11) | copy-start | bytes 6291460
  7.2 17.0 %copy-start.20 = (bf16[1,256,512]{2,1,0:T(8,128)(2,1)S(1)}, bf16[1,256,512]{2,1,0:T(8,128)(2,1)}, u32[]{:S(2)}) copy-start(bf16[1,256,512]{2,1,0:T(8,128)(2,1)} %param.16) | copy-start | bytes 786436
  7.2 1082.4 %reduce-scatter.4.cloned.1.call-start = ((), (), s32[]{:S(2)}) async-start(), calls=%async_computation.1 | async-start | bytes 25362432
  9.2 44.8 %collective-permute-start.1 = (bf16[256,512]{0,1:T(8,128)(2,1)}, bf16[256,512]{0,1:T(8,128)(2,1)}, u32[]{:S(2)}, u32[]{:S(2)}) collective-permute-start(bf16[256,512]{0,1:T(8,128)(2,1)} %bitcast.29), channel_id=1, source_target_pairs={{0,1},{1,2},{2,3},{3,4},{4,5},{5,6},{6,7},{7,0},{8,9},{9,10},{10,1... | collective-permute-start | bytes 786440 | tf_op jit(solution)/shard_map/ppermute | solution.py:15
  14.3 37.3 %collective-permute-start = (bf16[256,512]{0,1:T(8,128)(2,1)S(1)}, bf16[256,512]{0,1:T(8,128)(2,1)}, u32[]{:S(2)}, u32[]{:S(2)}) collective-permute-start(bf16[256,512]{0,1:T(8,128)(2,1)S(1)} %bitcast.223), channel_id=1, source_target_pairs={{0,1},{1,2},{2,3},{3,4},{4,5},{5,6},{6,7},{7,0},{8,9},{9,10},{10,1... | collective-permute-start | bytes 786440 | tf_op jit(solution)/shard_map/ppermute | solution.py:15
  27.0 11.2 %copy-start.17 = (bf16[256,4,128]{2,1,0:T(4,128)(2,1)S(1)}, bf16[256,4,128]{2,1,0:T(4,128)(2,1)}, u32[]{:S(2)}) copy-start(bf16[256,4,128]{2,1,0:T(4,128)(2,1)} %reshape_squeeze.13) | copy-start | bytes 786436
  37.2 1.0 copy-start.4
  41.7 47.7 %collective-permute-start.14 = (f32[256,512]{1,0:T(8,128)}, f32[256,512]{1,0:T(8,128)}, u32[]{:S(2)}, u32[]{:S(2)}) collective-permute-start(f32[256,512]{1,0:T(8,128)} %copy.250), channel_id=1, source_target_pairs={{0,1},{1,2},{2,3},{3,4},{4,5},{5,6},{6,7},{7,0},{8,9},{9,10},{10,1... | collective-permute-start | bytes 1572872 | tf_op jit(solution)/shard_map/ppermute | solution.py:15
  49.9 43.4 %collective-permute-start.22 = (f32[256,512]{1,0:T(8,128)}, f32[256,512]{1,0:T(8,128)}, u32[]{:S(2)}, u32[]{:S(2)}) collective-permute-start(f32[256,512]{1,0:T(8,128)} %copy.266), channel_id=1, source_target_pairs={{0,1},{1,2},{2,3},{3,4},{4,5},{5,6},{6,7},{7,0},{8,9},{9,10},{10,1... | collective-permute-start | bytes 1572872 | tf_op jit(solution)/shard_map/ppermute | solution.py:15
  60.5 24.1 %collective-permute-start.3 = (bf16[256,512]{0,1:T(8,128)(2,1)}, bf16[256,512]{0,1:T(8,128)(2,1)}, u32[]{:S(2)}, u32[]{:S(2)}) collective-permute-start(bf16[256,512]{0,1:T(8,128)(2,1)} %collective-permute-done.1), channel_id=1, source_target_pairs={{0,1},{1,2},{2,3},{3,4},{4,5},{5,6},{6,7},{7,0},{8,9},{9,10},{10,1... | collective-permute-start | bytes 786440 | tf_op jit(solution)/shard_map/ppermute | solution.py:15
  64.4 16.7 %collective-permute-start.2 = (bf16[256,512]{0,1:T(8,128)(2,1)}, bf16[256,512]{0,1:T(8,128)(2,1)S(1)}, u32[]{:S(2)}, u32[]{:S(2)}) collective-permute-start(bf16[256,512]{0,1:T(8,128)(2,1)} %collective-permute-done), channel_id=1, source_target_pairs={{0,1},{1,2},{2,3},{3,4},{4,5},{5,6},{6,7},{7,0},{8,9},{9,10},{10,1... | collective-permute-start | bytes 786440 | tf_op jit(solution)/shard_map/ppermute | solution.py:15
  82.3 1.0 copy-start.5
  89.3 11.9 %copy-start.8 = (f32[4,256,128]{1,2,0:T(8,128)S(1)}, f32[4,256,128]{1,2,0:T(8,128)}, u32[]{:S(2)}) copy-start(f32[4,256,128]{1,2,0:T(8,128)} %convolution_add_fusion.6) | copy-start | bytes 1572868
  91.5 38.5 %copy-start.23 = (pred[256,256]{1,0:T(8,128)(4,1)S(1)}, pred[256,256]{1,0:T(8,128)(4,1)}, u32[]{:S(2)}) copy-start(pred[256,256]{1,0:T(8,128)(4,1)} %get-tuple-element.76) | copy-start | bytes 196612
  91.5 69.9 %collective-permute-start.15 = (f32[256,512]{1,0:T(8,128)}, f32[256,512]{1,0:T(8,128)}, u32[]{:S(2)}, u32[]{:S(2)}) collective-permute-start(f32[256,512]{1,0:T(8,128)} %add.300), channel_id=1, source_target_pairs={{0,1},{1,2},{2,3},{3,4},{4,5},{5,6},{6,7},{7,0},{8,9},{9,10},{10,1... | collective-permute-start | bytes 1572872 | tf_op jit(solution)/shard_map/ppermute | solution.py:15
  95.3 68.2 %collective-permute-start.23 = (f32[256,512]{1,0:T(8,128)}, f32[256,512]{1,0:T(8,128)}, u32[]{:S(2)}, u32[]{:S(2)}) collective-permute-start(f32[256,512]{1,0:T(8,128)} %add.307), channel_id=1, source_target_pairs={{0,1},{1,2},{2,3},{3,4},{4,5},{5,6},{6,7},{7,0},{8,9},{9,10},{10,1... | collective-permute-start | bytes 1572872 | tf_op jit(solution)/shard_map/ppermute | solution.py:15
  96.9 34.6 %collective-permute-start.5 = (bf16[256,512]{0,1:T(8,128)(2,1)}, bf16[256,512]{0,1:T(8,128)(2,1)}, u32[]{:S(2)}, u32[]{:S(2)}) collective-permute-start(bf16[256,512]{0,1:T(8,128)(2,1)} %collective-permute-done.3), channel_id=1, source_target_pairs={{0,1},{1,2},{2,3},{3,4},{4,5},{5,6},{6,7},{7,0},{8,9},{9,10},{10,1... | collective-permute-start | bytes 786440 | tf_op jit(solution)/shard_map/ppermute | solution.py:15
  99.9 30.1 %collective-permute-start.4 = (bf16[256,512]{0,1:T(8,128)(2,1)S(1)}, bf16[256,512]{0,1:T(8,128)(2,1)S(1)}, u32[]{:S(2)}, u32[]{:S(2)}) collective-permute-start(bf16[256,512]{0,1:T(8,128)(2,1)S(1)} %collective-permute-done.2), channel_id=1, source_target_pairs={{0,1},{1,2},{2,3},{3,4},{4,5},{5,6},{6,7},{7,0},{8,9},{9,10},{10,1... | collective-permute-start | bytes 786440 | tf_op jit(solution)/shard_map/ppermute | solution.py:15
  130.0 2.8 copy-start.19
  137.9 18.7 %collective-permute-start.7 = (bf16[256,512]{0,1:T(8,128)(2,1)}, bf16[256,512]{0,1:T(8,128)(2,1)}, u32[]{:S(2)}, u32[]{:S(2)}) collective-permute-start(bf16[256,512]{0,1:T(8,128)(2,1)} %collective-permute-done.5), channel_id=1, source_target_pairs={{0,1},{1,2},{2,3},{3,4},{4,5},{5,6},{6,7},{7,0},{8,9},{9,10},{10,1... | collective-permute-start | bytes 786440 | tf_op jit(solution)/shard_map/ppermute | solution.py:15
  137.9 15.2 %collective-permute-start.6 = (bf16[256,512]{0,1:T(8,128)(2,1)}, bf16[256,512]{0,1:T(8,128)(2,1)S(1)}, u32[]{:S(2)}, u32[]{:S(2)}) collective-permute-start(bf16[256,512]{0,1:T(8,128)(2,1)} %copy-done.19), channel_id=1, source_target_pairs={{0,1},{1,2},{2,3},{3,4},{4,5},{5,6},{6,7},{7,0},{8,9},{9,10},{10,1... | collective-permute-start | bytes 786440 | tf_op jit(solution)/shard_map/ppermute | solution.py:15
  154.4 1.0 copy-start.6
  161.4 9.7 copy-start.9
  163.5 36.9 %copy-start.22 = (pred[256,256]{1,0:T(8,128)(4,1)S(1)}, pred[256,256]{1,0:T(8,128)(4,1)}, u32[]{:S(2)}) copy-start(pred[256,256]{1,0:T(8,128)(4,1)} %get-tuple-element.78) | copy-start | bytes 196612
  163.5 47.2 %collective-permute-start.16 = (f32[256,512]{1,0:T(8,128)}, f32[256,512]{1,0:T(8,128)}, u32[]{:S(2)}, u32[]{:S(2)}) collective-permute-start(f32[256,512]{1,0:T(8,128)} %add.301), channel_id=1, source_target_pairs={{0,1},{1,2},{2,3},{3,4},{4,5},{5,6},{6,7},{7,0},{8,9},{9,10},{10,1... | collective-permute-start | bytes 1572872 | tf_op jit(solution)/shard_map/ppermute | solution.py:15
  165.6 47.1 %collective-permute-start.24 = (f32[256,512]{1,0:T(8,128)}, f32[256,512]{1,0:T(8,128)}, u32[]{:S(2)}, u32[]{:S(2)}) collective-permute-start(f32[256,512]{1,0:T(8,128)} %add.308), channel_id=1, source_target_pairs={{0,1},{1,2},{2,3},{3,4},{4,5},{5,6},{6,7},{7,0},{8,9},{9,10},{10,1... | collective-permute-start | bytes 1572872 | tf_op jit(solution)/shard_map/ppermute | solution.py:15
  166.5 35.4 %collective-permute-start.9 = (bf16[256,512]{0,1:T(8,128)(2,1)}, bf16[256,512]{0,1:T(8,128)(2,1)}, u32[]{:S(2)}, u32[]{:S(2)}) collective-permute-start(bf16[256,512]{0,1:T(8,128)(2,1)} %collective-permute-done.7), channel_id=1, source_target_pairs={{0,1},{1,2},{2,3},{3,4},{4,5},{5,6},{6,7},{7,0},{8,9},{9,10},{10,1... | collective-permute-start | bytes 786440 | tf_op jit(solution)/shard_map/ppermute | solution.py:15
  167.7 32.8 %collective-permute-start.8 = (bf16[256,512]{0,1:T(8,128)(2,1)S(1)}, bf16[256,512]{0,1:T(8,128)(2,1)S(1)}, u32[]{:S(2)}, u32[]{:S(2)}) collective-permute-start(bf16[256,512]{0,1:T(8,128)(2,1)S(1)} %collective-permute-done.6), channel_id=1, source_target_pairs={{0,1},{1,2},{2,3},{3,4},{4,5},{5,6},{6,7},{7,0},{8,9},{9,10},{10,1... | collective-permute-start | bytes 786440 | tf_op jit(solution)/shard_map/ppermute | solution.py:15
  200.4 2.8 copy-start.18
  208.3 2.4 copy-start.13
  208.3 4.3 copy-start.11
  208.3 21.3 %collective-permute-start.11 = (bf16[256,512]{0,1:T(8,128)(2,1)}, bf16[256,512]{0,1:T(8,128)(2,1)}, u32[]{:S(2)}, u32[]{:S(2)}) collective-permute-start(bf16[256,512]{0,1:T(8,128)(2,1)} %collective-permute-done.9), channel_id=1, source_target_pairs={{0,1},{1,2},{2,3},{3,4},{4,5},{5,6},{6,7},{7,0},{8,9},{9,10},{10,1... | collective-permute-start | bytes 786440 | tf_op jit(solution)/shard_map/ppermute | solution.py:15
  208.3 18.6 %collective-permute-start.10 = (bf16[256,512]{0,1:T(8,128)(2,1)}, bf16[256,512]{0,1:T(8,128)(2,1)S(1)}, u32[]{:S(2)}, u32[]{:S(2)}) collective-permute-start(bf16[256,512]{0,1:T(8,128)(2,1)} %copy-done.18), channel_id=1, source_target_pairs={{0,1},{1,2},{2,3},{3,4},{4,5},{5,6},{6,7},{7,0},{8,9},{9,10},{10,1... | collective-permute-start | bytes 786440 | tf_op jit(solution)/shard_map/ppermute | solution.py:15
  212.7 25.7 %collective-permute-start.17 = (f32[256,512]{1,0:T(8,128)}, f32[256,512]{1,0:T(8,128)}, u32[]{:S(2)}, u32[]{:S(2)}) collective-permute-start(f32[256,512]{1,0:T(8,128)} %add.302), channel_id=1, source_target_pairs={{0,1},{1,2},{2,3},{3,4},{4,5},{5,6},{6,7},{7,0},{8,9},{9,10},{10,1... | collective-permute-start | bytes 1572872 | tf_op jit(solution)/shard_map/ppermute | solution.py:15
  214.6 34.9 %collective-permute-start.25 = (f32[256,512]{1,0:T(8,128)}, f32[256,512]{1,0:T(8,128)}, u32[]{:S(2)}, u32[]{:S(2)}) collective-permute-start(f32[256,512]{1,0:T(8,128)} %add.309), channel_id=1, source_target_pairs={{0,1},{1,2},{2,3},{3,4},{4,5},{5,6},{6,7},{7,0},{8,9},{9,10},{10,1... | collective-permute-start | bytes 1572872 | tf_op jit(solution)/shard_map/ppermute | solution.py:15
  227.4 1.0 copy-start.7
  229.6 19.9 %copy-start.10 = (f32[256,512]{1,0:T(8,128)S(1)}, f32[256,512]{1,0:T(8,128)}, u32[]{:S(2)}) copy-start(f32[256,512]{1,0:T(8,128)} %copy.274) | copy-start | bytes 1572868
  240.4 20.4 %collective-permute-start.18 = (f32[256,512]{1,0:T(8,128)}, f32[256,512]{1,0:T(8,128)}, u32[]{:S(2)}, u32[]{:S(2)}) collective-permute-start(f32[256,512]{1,0:T(8,128)} %add.303), channel_id=1, source_target_pairs={{0,1},{1,2},{2,3},{3,4},{4,5},{5,6},{6,7},{7,0},{8,9},{9,10},{10,1... | collective-permute-start | bytes 1572872 | tf_op jit(solution)/shard_map/ppermute | solution.py:15
  251.5 20.6 %collective-permute-start.26 = (f32[256,512]{1,0:T(8,128)}, f32[256,512]{1,0:T(8,128)}, u32[]{:S(2)}, u32[]{:S(2)}) collective-permute-start(f32[256,512]{1,0:T(8,128)} %add.310), channel_id=1, source_target_pairs={{0,1},{1,2},{2,3},{3,4},{4,5},{5,6},{6,7},{7,0},{8,9},{9,10},{10,1... | collective-permute-start | bytes 1572872 | tf_op jit(solution)/shard_map/ppermute | solution.py:15
  254.5 6.2 copy-start.15
  254.6 17.5 %copy-start.12 = (f32[256,512]{1,0:T(8,128)S(1)}, f32[256,512]{1,0:T(8,128)}, u32[]{:S(2)}) copy-start(f32[256,512]{1,0:T(8,128)} %copy.276) | copy-start | bytes 1572868
  254.6 53.1 %collective-permute-start.13 = (bf16[256,512]{0,1:T(8,128)(2,1)}, bf16[256,512]{0,1:T(8,128)(2,1)}, u32[]{:S(2)}, u32[]{:S(2)}) collective-permute-start(bf16[256,512]{0,1:T(8,128)(2,1)} %collective-permute-done.11), channel_id=1, source_target_pairs={{0,1},{1,2},{2,3},{3,4},{4,5},{5,6},{6,7},{7,0},{8,9},{9,10},{10,1... | collective-permute-start | bytes 786440 | tf_op jit(solution)/shard_map/ppermute | solution.py:15
  254.6 28.6 %collective-permute-start.12 = (bf16[256,512]{0,1:T(8,128)(2,1)S(1)}, bf16[256,512]{0,1:T(8,128)(2,1)S(1)}, u32[]{:S(2)}, u32[]{:S(2)}) collective-permute-start(bf16[256,512]{0,1:T(8,128)(2,1)S(1)} %collective-permute-done.10), channel_id=1, source_target_pairs={{0,1},{1,2},{2,3},{3,4},{4,5},{5,6},{6,7},{7,0},{8,9},{9,10},{10,1... | collective-permute-start | bytes 786440 | tf_op jit(solution)/shard_map/ppermute | solution.py:15
  262.7 31.8 %collective-permute-start.19 = (f32[256,512]{1,0:T(8,128)}, f32[256,512]{1,0:T(8,128)}, u32[]{:S(2)}, u32[]{:S(2)}) collective-permute-start(f32[256,512]{1,0:T(8,128)} %add.304), channel_id=1, source_target_pairs={{0,1},{1,2},{2,3},{3,4},{4,5},{5,6},{6,7},{7,0},{8,9},{9,10},{10,1... | collective-permute-start | bytes 1572872 | tf_op jit(solution)/shard_map/ppermute | solution.py:15
  273.9 31.8 %collective-permute-start.27 = (f32[256,512]{1,0:T(8,128)}, f32[256,512]{1,0:T(8,128)}, u32[]{:S(2)}, u32[]{:S(2)}) collective-permute-start(f32[256,512]{1,0:T(8,128)} %add.311), channel_id=1, source_target_pairs={{0,1},{1,2},{2,3},{3,4},{4,5},{5,6},{6,7},{7,0},{8,9},{9,10},{10,1... | collective-permute-start | bytes 1572872 | tf_op jit(solution)/shard_map/ppermute | solution.py:15
  283.1 2.5 copy-start.21
  283.6 1.0 copy-start.2
  284.6 21.2 %copy-start.14 = (f32[256,512]{1,0:T(8,128)S(1)}, f32[256,512]{1,0:T(8,128)}, u32[]{:S(2)}) copy-start(f32[256,512]{1,0:T(8,128)} %copy.278) | copy-start | bytes 1572868
  287.7 20.0 %copy-start.3 = (f32[4,256,256]{2,1,0:T(8,128)S(1)}, f32[4,256,256]{2,1,0:T(8,128)}, u32[]{:S(2)}) copy-start(f32[4,256,256]{2,1,0:T(8,128)} %copy-done.2) | copy-start | bytes 3145732
  296.6 20.4 %collective-permute-start.20 = (f32[256,512]{1,0:T(8,128)}, f32[256,512]{1,0:T(8,128)}, u32[]{:S(2)}, u32[]{:S(2)}) collective-permute-start(f32[256,512]{1,0:T(8,128)} %add.305), channel_id=1, source_target_pairs={{0,1},{1,2},{2,3},{3,4},{4,5},{5,6},{6,7},{7,0},{8,9},{9,10},{10,1... | collective-permute-start | bytes 1572872 | tf_op jit(solution)/shard_map/ppermute | solution.py:15
  307.7 18.4 %collective-permute-start.28 = (f32[256,512]{1,0:T(8,128)}, f32[256,512]{1,0:T(8,128)}, u32[]{:S(2)}, u32[]{:S(2)}) collective-permute-start(f32[256,512]{1,0:T(8,128)} %add.312), channel_id=1, source_target_pairs={{0,1},{1,2},{2,3},{3,4},{4,5},{5,6},{6,7},{7,0},{8,9},{9,10},{10,1... | collective-permute-start | bytes 1572872 | tf_op jit(solution)/shard_map/ppermute | solution.py:15
  310.0 16.1 %copy-start.16 = (f32[256,512]{1,0:T(8,128)S(1)}, f32[256,512]{1,0:T(8,128)}, u32[]{:S(2)}) copy-start(f32[256,512]{1,0:T(8,128)} %copy.280) | copy-start | bytes 1572868
  318.9 12.6 %collective-permute-start.21 = (bf16[256,512]{1,0:T(8,128)(2,1)}, bf16[256,512]{1,0:T(8,128)(2,1)S(1)}, u32[]{:S(2)}, u32[]{:S(2)}) collective-permute-start(bf16[256,512]{1,0:T(8,128)(2,1)} %add.306), channel_id=1, source_target_pairs={{0,1},{1,2},{2,3},{3,4},{4,5},{5,6},{6,7},{7,0},{8,9},{9,10},{10,1... | collective-permute-start | bytes 786440 | tf_op jit(solution)/shard_map/ppermute | solution.py:15
  327.9 10.2 collective-permute-start.29
  372.9 718.1 %copy-start.1 = (bf16[1,256,4096]{2,1,0:T(8,128)(2,1)S(1)}, bf16[1,256,4096]{2,1,0:T(8,128)(2,1)}, u32[]{:S(2)}) copy-start(bf16[1,256,4096]{2,1,0:T(8,128)(2,1)} %param.11) | copy-start | bytes 6291460
Sparse Core Ops, SparseCore 0:
  373.1 716.4 reduce-scatter.3
where the time goes:
time: 1100 us
  waiting for transfers between devices  880 us (80%)
  local copies, waits for them, and re-layouts  69.7 us (6%)
  matrix products  55.7 us (5%)
  other arithmetic  44.7 us (4%)
  starting transfers between devices  33.3 us (3%)
  between operations  14.5 us (1%)
    unnamed x2, waiting for transfers between devices  716 us
    ppermute x30, waiting for transfers between devices, shifted(): lax.ppermute(array, axis, [(i, (i + by) % peers) for i in range(peers)])  164 us
    unnamed x53, local copies, waits for them, and re-layouts  33.9 us
    ppermute x30, starting transfers between devices, shifted(): lax.ppermute(array, axis, [(i, (i + by) % peers) for i in range(peers)])  33.3 us
    reshape x16, local copies, waits for them, and re-layouts, column_part(): return result.reshape(matrix.shape[2], HEADS * HEAD_DIM)  29.7 us
  transfers between devices with their start and end apart: 31, of which 17 were waited for; matrix products, arithmetic and copies ran while one was open for 12% of the time, Pallas kernels for 0%

commit v1 on v0

v1 whole, which is shorter than its diff:
```python
import functools
import math

import jax
import jax.numpy as jnp
from jax import lax
from jax.experimental import pallas as pl
from jax.experimental.pallas import tpu as pltpu
from jax.sharding import PartitionSpec as P

HEADS = 4
HD = 128
TOK = 256
LOG2E = math.log2(math.e)
SCALE = 1.0 / math.sqrt(HD)
HIDDEN = 1e30
MESH = pl.DeviceIdType.MESH
F32 = jnp.float32
BF16 = jnp.bfloat16
ANY = pl.BlockSpec(memory_space=pl.ANY)
VM = pl.BlockSpec(memory_space=pltpu.VMEM)
SM = pl.BlockSpec(memory_space=pltpu.SMEM)


def place():
    dp = lax.axis_index("dp")
    ctx = lax.axis_index("ctx")
    core = lax.rem(dp, 2)
    x = lax.rem(dp // 2, 4)
    z_lo = dp // 8
    y = ctx // 2
    z_hi = lax.rem(ctx, 2)
    return core, x, y, z_lo, z_hi, dp, ctx


def greet(devices):
    barrier = pltpu.get_barrier_semaphore()
    for d in devices:
        pl.semaphore_signal(barrier, inc=1, device_id=d, device_id_type=MESH)
    return lambda: pl.semaphore_wait(barrier, len(devices))


def remote(src, dst, send, recv, device):
    return pltpu.make_async_remote_copy(
        src_ref=src, dst_ref=dst, send_sem=send, recv_sem=recv,
        device_id=device, device_id_type=MESH,
    )


def tile_rows(labels, layout, ctx):
    n0 = jnp.int32(0)
    n1 = jnp.int32(0)
    for j in range(16):
        lab = labels[0, j]
        n0 = n0 + jnp.where(lab == 0, 1, 0)
        n1 = n1 + jnp.where(lab == 1, 1, 0)
    n2 = 16 - n0 - n1
    out = []
    for t in range(2):
        lab = labels[0, layout[0, 2 * ctx + t]]
        own = jnp.where(lab == 1, n1, jnp.where(lab == 2, n2, 0))
        count = ((n0 + own) * 128).astype(F32)
        out.append((lab, jnp.log(jnp.full((1, 128), count, F32))))
    return out


def spread_kernel(
    labels, layout, lse, do_v, o_v, q, k, v, do, x_in,
    qo, doo, ko, vo, auxo, xo,
    aux, send, recv, fsend, frecv, xsend, xrecv,
):
    core, x, y, z_lo, z_hi, dp, ctx = place()
    base = dp - core
    targets = [(base + 1 - z_hi, h * 2 + core) for h in range(4)]
    sources = [(base + z_hi, s * 2 + 1 - core) for s in range(4)]
    sibling = (base + 1 - core, ctx)
    ready = greet(targets + sources + [sibling])

    tiles = tile_rows(labels, layout, ctx)
    labs = jnp.concatenate(
        [jnp.full((1, 128), lab, jnp.int32) for lab, _ in tiles], axis=1
    )
    logs = jnp.concatenate([lg for _, lg in tiles], axis=1)
    for h in range(HEADS):
        cols = slice(h * HD, (h + 1) * HD)
        prod = do_v[0, :, cols].astype(F32) * o_v[0, :, cols].astype(F32)
        delta = jnp.sum(prod.T, axis=0, keepdims=True)
        ln = (logs + lse[0, h : h + 1, :]) * LOG2E
        aux[h, 0:1, :] = ln
        aux[h, 1:2, :] = jnp.where(labs == 1, ln, HIDDEN)
        aux[h, 2:3, :] = jnp.where(labs == 2, ln, HIDDEN)
        aux[h, 3:4, :] = delta
        aux[h, 4:5, :] = labs.astype(F32)
        aux[h, 5:8, :] = jnp.zeros((3, TOK), F32)

    ready()
    xs = []
    for i in range(8):
        c = remote(
            x_in.at[0, :, pl.ds(pl.multiple_of((2 * i + 1 - core) * 256, 256), 256)],
            xo.at[i], xsend.at[i], xrecv.at[i], sibling,
        )
        c.start()
        xs.append(c)
    copies = []
    arrays = ((q, qo), (do, doo), (None, auxo), (k, ko), (v, vo))
    for n, (src, dst) in enumerate(arrays):
        for h in range(HEADS):
            if src is None:
                s = aux.at[h]
            else:
                s = src.at[0, :, h * HD : (h + 1) * HD]
            c = remote(s, dst.at[y], send.at[n, h], recv.at[n, y], targets[h])
            c.start()
            copies.append(c)

    def arrived(n, s):
        dst = arrays[n][1].at[s]
        remote(dst, dst, send.at[n, s], recv.at[n, s], sibling).wait_recv()

    fwd = []
    for s in range(4):
        for n in range(3):
            arrived(n, s)
            dst = arrays[n][1]
            c = remote(dst.at[s], dst.at[4 + s], fsend.at[n, s], frecv.at[n, s], sibling)
            c.start()
            fwd.append(c)
    for s in range(4):
        arrived(3, s)
        arrived(4, s)
    for c in copies:
        c.wait_send()
    for c in fwd:
        c.wait()
    for c in xs:
        c.wait()


def spread(labels, layout, lse, q, k, v, o, do, x_in):
    blk = lambda n: jax.ShapeDtypeStruct((n, TOK, HD), BF16)
    return pl.pallas_call(
        spread_kernel,
        out_shape=(
            blk(8), blk(8), blk(4), blk(4),
            jax.ShapeDtypeStruct((8, 8, TOK), F32),
            jax.ShapeDtypeStruct((8, TOK, 256), BF16),
        ),
        in_specs=[SM, SM, VM, VM, VM, ANY, ANY, ANY, ANY, ANY],
        out_specs=(ANY,) * 6,
        scratch_shapes=[
            pltpu.VMEM((4, 8, TOK), F32),
            pltpu.SemaphoreType.DMA((5, 4)),
            pltpu.SemaphoreType.DMA((5, 4)),
            pltpu.SemaphoreType.DMA((3, 4)),
            pltpu.SemaphoreType.DMA((3, 4)),
            pltpu.SemaphoreType.DMA((8,)),
            pltpu.SemaphoreType.DMA((8,)),
        ],
        compiler_params=pltpu.CompilerParams(collective_id=0, has_side_effects=True),
        name="spread",
    )(labels, layout, lse, do, o, q, k, v, do, x_in)


def dot_t(a, b):
    return lax.dot_general(a, b, (((1,), (1,)), ((), ())), preferred_element_type=F32)


def dot_n(a, b):
    return lax.dot_general(a, b, (((1,), (0,)), ((), ())), preferred_element_type=F32)


def dot_l(a, b):
    return lax.dot_general(a, b, (((0,), (0,)), ((), ())), preferred_element_type=F32)


def attention_kernel(q, do, k, v, aux, dk, dv, dq_out, dk_acc, dv_acc, p_s, ds_s):
    dk_acc[...] = jnp.zeros_like(dk_acc)
    dv_acc[...] = jnp.zeros_like(dv_acc)
    k_all = k[...].reshape(4 * TOK, HD)
    v_all = v[...].reshape(4 * TOK, HD)

    def step(c, carry):
        qc = q[c]
        doc = do[c]
        s = dot_t(k_all, qc)
        d = dot_t(v_all, doc)
        rows = aux[c]
        delta = rows[3:4, :]
        for t in range(8):
            part = slice(t * 128, (t + 1) * 128)
            lab = aux[t // 2, 4:5, (t % 2) * 128 : (t % 2) * 128 + 1]
            row = jnp.where(
                lab == 0.0, rows[0:1, :], jnp.where(lab == 1.0, rows[1:2, :], rows[2:3, :])
            )
            p = jnp.exp2(s[part] * (SCALE * LOG2E) - row)
            p_s[part, :] = p.astype(BF16)
            ds_s[part, :] = (p * (d[part] - delta) * SCALE).astype(BF16)
        p_b = p_s[...]
        ds_b = ds_s[...]
        dv_acc[...] += dot_n(p_b, doc)
        dk_acc[...] += dot_n(ds_b, qc)
        dq = dot_l(ds_b, k_all)
        dq_out[c] = dq.astype(BF16)
        return carry

    lax.fori_loop(0, 8, step, 0)
    dk[...] = dk_acc[...].astype(BF16).reshape(4, TOK, HD)
    dv[...] = dv_acc[...].astype(BF16).reshape(4, TOK, HD)


def attention(q, do, k, v, aux):
    blk = lambda n: jax.ShapeDtypeStruct((n, TOK, HD), BF16)

    return pl.pallas_call(
        attention_kernel,
        out_shape=(blk(4), blk(4), blk(8)),
        in_specs=[VM] * 5,
        out_specs=(VM,) * 3,
        scratch_shapes=[
            pltpu.VMEM((1024, HD), F32),
            pltpu.VMEM((1024, HD), F32),
            pltpu.VMEM((1024, TOK), BF16),
            pltpu.VMEM((1024, TOK), BF16),
        ],
        name="attention",
    )(q, do, k, v, aux)


def collect_kernel(
    dk, dv, dq, dq_v, g,
    other, total, osend, orecv, send, recv, fsend, frecv,
):
    core, x, y, z_lo, z_hi, dp, ctx = place()
    base = dp - core
    targets = [(base + 1 - z_hi, h * 2 + core) for h in range(4)]
    owners = [(base + z_hi, s * 2 + 1 - core) for s in range(4)]
    sibling = (base + 1 - core, ctx)
    greet(targets + owners + [sibling])()

    swap = remote(dq.at[pl.ds(4, 4)], other, osend, orecv, sibling)
    swap.start()
    copies = []

    def give(t, s, src):
        c = remote(src, g.at[0, t, y], send.at[t, s], recv.at[t, y], owners[s])
        c.start()
        copies.append(c)

    for s in range(4):
        give(1, s, dk.at[s])
    for s in range(4):
        give(2, s, dv.at[s])
    swap.wait()
    for s in range(4):
        total[s] = (dq_v[s].astype(F32) + other[s].astype(F32)).astype(BF16)
    for s in range(4):
        give(0, s, total.at[s])
    fwd = []
    for t in (1, 2, 0):
        for h in range(4):
            piece = g.at[0, t, h]
            remote(piece, piece, send.at[t, h], recv.at[t, h], sibling).wait_recv()
            c = remote(piece, g.at[1, t, h], fsend.at[t, h], frecv.at[t, h], sibling)
            c.start()
            fwd.append(c)
    for c in copies:
        c.wait_send()
    for c in fwd:
        c.wait()


def collect(dk, dv, dq):
    return pl.pallas_call(
        collect_kernel,
        out_shape=jax.ShapeDtypeStruct((2, 3, 4, TOK, HD), BF16),
        in_specs=[ANY, ANY, ANY, VM],
        out_specs=ANY,
        scratch_shapes=[
            pltpu.VMEM((4, TOK, HD), BF16),
            pltpu.VMEM((4, TOK, HD), BF16),
            pltpu.SemaphoreType.DMA,
            pltpu.SemaphoreType.DMA,
            pltpu.SemaphoreType.DMA((3, 4)),
            pltpu.SemaphoreType.DMA((3, 4)),
            pltpu.SemaphoreType.DMA((3, 4)),
            pltpu.SemaphoreType.DMA((3, 4)),
        ],
        compiler_params=pltpu.CompilerParams(collective_id=1, has_side_effects=True),
        name="collect",
    )(dk, dv, dq, dq)


def project_kernel(core, xa, xb, g, part, gq, gk, gv, rhs):
    i = pl.program_id(0)

    @pl.when(i == 0)
    def _():
        for t, out in enumerate((gq, gk, gv)):
            for h in range(4):
                for c in range(2):
                    rhs[c * TOK : (c + 1) * TOK, (t * 4 + h) * HD : (t * 4 + h + 1) * HD] = g[c, t, h]
                out[0, :, h * HD : (h + 1) * HD] = g[0, t, h]

    lhs = jnp.concatenate([xa[0].T, xb[0].T], axis=1)
    for n in range(6):
        res = dot_n(lhs, rhs[:, n * 256 : (n + 1) * 256])
        part[n, 0] = res.astype(BF16).reshape(8, 32, 256)


def project(core, x_in, xo, g):
    grad = jax.ShapeDtypeStruct((1, TOK, HEADS * HD), BF16)
    gspec = pl.BlockSpec((1, TOK, HEADS * HD), lambda i, c: (0, 0, 0))
    return pl.pallas_call(
        project_kernel,
        out_shape=(jax.ShapeDtypeStruct((6, 8, 8, 32, 256), BF16), grad, grad, grad),
        grid_spec=pltpu.PrefetchScalarGridSpec(
            num_scalar_prefetch=1,
            grid=(8,),
            in_specs=[
                pl.BlockSpec((1, TOK, 256), lambda i, c: (0, 0, 2 * i + c[0])),
                pl.BlockSpec((1, TOK, 256), lambda i, c: (i, 0, 0)),
                pl.BlockSpec((2, 3, 4, TOK, HD), lambda i, c: (0, 0, 0, 0, 0)),
            ],
            out_specs=(
                pl.BlockSpec((6, 1, 8, 32, 256), lambda i, c: (0, i, 0, 0, 0)),
                gspec, gspec, gspec,
            ),
            scratch_shapes=[pltpu.VMEM((2 * TOK, 1536), BF16)],
        ),
        name="project",
    )(core, x_in, xo, g)


ORDERS = ("xyz", "yzx", "zxy")
SIZES = {"l": 2, "x": 4, "y": 4, "h": 2}


def reduce_kernel(part, out, *scratch):
    core, x, y, z_lo, z_hi, dp, ctx = place()
    z = z_hi * 2 + z_lo
    here = {"x": x, "y": y, "z": z}

    def device(axis, by):
        c = dict(here)
        c[axis] = lax.rem(c[axis] + by + 4, 4)
        return (lax.rem(c["z"], 2) * 8 + c["x"] * 2 + core, c["y"] * 2 + c["z"] // 2)

    neighbours = [device(a, by) for a in "xyz" for by in (1, -1)]
    ready = greet(neighbours)
    bufs = scratch[:27]
    send, recv = scratch[27:]
    ready()

    def pick(ref, dims, axis, coord):
        if axis == "z":
            want = {"l": lax.rem(coord, 2), "h": coord // 2}
        else:
            want = {axis: coord}
        idx = tuple(want[d] if d in want else slice(None) for d in dims)
        return idx, "".join(d for d in dims if d not in want)

    state = []
    for n in range(3):
        state.append(((lambda half, n=n: part.at[2 * n + half]), "lxyh"))

    for stage in range(3):
        jobs = []
        for n in range(3):
            axis = ORDERS[n][stage]
            got, comb, tot = bufs[(stage * 3 + n) * 3 : (stage * 3 + n) * 3 + 3]
            view, dims = state[n]
            a = here[axis]
            right = lax.rem(a + 1, 4)
            left = lax.rem(a + 3, 4)
            opp = lax.rem(a + 2, 4)
            dev_r, dev_l = device(axis, 1), device(axis, -1)
            ss, rs = send.at[stage, n], recv.at[stage, n]

            def piece(half, coord, view=view, dims=dims, axis=axis):
                idx, _ = pick(None, dims, axis, coord)
                return view(half).at[idx]

            rest = pick(None, dims, axis, 0)[1]

            def job(msg, src, dev, got=got, ss=ss, rs=rs):
                return remote(src, got.at[msg], ss.at[msg], rs.at[msg], dev)

            first = [
                job(0, piece(0, opp), dev_r),
                job(1, piece(1, opp), dev_l),
                job(2, piece(1, right), dev_r),
                job(3, piece(0, left), dev_l),
            ]
            jobs.append((n, piece, first, job, got, comb, tot, rest, a, right, left, dev_r, dev_l))
        for m in range(4):
            for j in jobs:
                j[2][m].start()
        second = []
        for msg in (0, 1):
            for n, piece, first, job, got, comb, tot, rest, a, right, left, dev_r, dev_l in jobs:
                first[msg].wait_recv()
                mine = piece(msg, right if msg == 0 else left)
                comb[msg] = (got[msg].astype(F32) + mine[...].astype(F32)).astype(BF16)
                c = job(4 + msg, comb.at[msg], dev_r if msg == 0 else dev_l)
                c.start()
                second.append(c)
        for n, piece, first, job, got, comb, tot, rest, a, right, left, dev_r, dev_l in jobs:
            first[3].wait_recv()
            second[n].wait_recv()
            first[2].wait_recv()
            second[3 + n].wait_recv()
            for half, raw, summed in ((0, 3, 4), (1, 2, 5)):
                total = (
                    piece(half, a)[...].astype(F32)
                    + got[raw].astype(F32)
                    + got[summed].astype(F32)
                )
                if stage < 2:
                    tot[half] = total.astype(BF16)
                else:
                    out[:, n * 512 + half * 256 : n * 512 + half * 256 + 256] = total
            state[n] = ((lambda half, tot=tot: tot.at[half]), rest)
        for j in jobs:
            for c in j[2]:
                c.wait_send()
        for c in second:
            c.wait_send()


def reduce(part):
    part = part.reshape(6, 2, 4, 4, 2, 32, 256)
    scratch = []
    dims = ["lxyh"] * 3
    for stage in range(3):
        for n in range(3):
            axis = ORDERS[n][stage]
            drop = "lh" if axis == "z" else axis
            rest = "".join(d for d in dims[n] if d not in drop)
            dims[n] = rest
            shape = tuple(SIZES[d] for d in rest) + (32, 256)
            scratch.append(pltpu.VMEM((6,) + shape, BF16))
            scratch.append(pltpu.VMEM((2,) + shape, BF16))
            scratch.append(pltpu.VMEM((2,) + shape, BF16))
    scratch += [pltpu.SemaphoreType.DMA((3, 3, 6)), pltpu.SemaphoreType.DMA((3, 3, 6))]
    return pl.pallas_call(
        reduce_kernel,
        out_shape=jax.ShapeDtypeStruct((32, 1536), F32),
        in_specs=[VM],
        out_specs=VM,
        scratch_shapes=scratch,
        compiler_params=pltpu.CompilerParams(collective_id=2, has_side_effects=True),
        name="reduce",
    )(part)


def per_device(inputs, queries, keys, values, attn_out, grad_out, lse_shift, labels, layout):
    q, do, k, v, aux, xo = spread(
        labels, layout, lse_shift, queries, keys, values, attn_out, grad_out, inputs
    )
    dk, dv, dq = attention(q, do, k, v, aux)
    g = collect(dk, dv, dq)
    core = lax.rem(lax.axis_index("dp"), 2).astype(jnp.int32).reshape(1)
    part, gq, gk, gv = project(core, inputs, xo, g)
    gw = reduce(part)
    return gq, gk, gv, gw


def solution(mesh):
    tok = P("dp", "ctx", None)
    return jax.shard_map(
        per_device,
        mesh=mesh,
        in_specs=(tok,) * 6 + (P("dp", None, "ctx"), P("dp", None), P("dp", None)),
        out_specs=(tok, tok, tok, P(("dp", "ctx"), None)),
        check_vma=False,
    )
```

time: 1100 us -> 105 us (0.10)
  waiting for transfers between devices: 880 us -> 0 us
  Pallas kernels: 0 us -> 102 us
  local copies, waits for them, and re-layouts: 69.7 us -> 1.62 us
  matrix products: 55.7 us -> 0 us
  other arithmetic: 44.7 us -> 0 us
  starting transfers between devices: 33.3 us -> 0 us
  between operations: 14.5 us -> 0.66 us
    unnamed x2 -> x0, waiting for transfers between devices: 716 us -> none
    ppermute x30 -> x0, waiting for transfers between devices: 164 us -> none  [shifted(): lax.ppermute(array, axis, [(i, (i + by) % peers) for i in range(peers)])]
    pallas_call x0 -> x5, Pallas kernels: none -> 102 us  [the longest x1 43.4 us: reduce(): pl.pallas_call(reduce_kernel, out_shape=jax.ShapeDtypeStruct((32, 1536),...]
    dot_general x41 -> x0, matrix products: 55.7 us -> none  [the longest x16 15.4 us: column_part(): jnp.einsum('hqk,qhd->khd', matrix, split_heads(query_rows), preferred_ele...]
    ppermute x30 -> x0, starting transfers between devices: 33.3 us -> none  [shifted(): lax.ppermute(array, axis, [(i, (i + by) % peers) for i in range(peers)])]
    unnamed x53 -> x1, local copies, waits for them, and re-layouts: 33.9 us -> 1.62 us
    reshape x16 -> x0, local copies, waits for them, and re-layouts: 29.7 us -> none  [column_part(): return result.reshape(matrix.shape[2], HEADS * HEAD_DIM)]
    add x16 -> x0, other arithmetic: 28.7 us -> none  [the longest x7 14.2 us: per_device(): moving_gk = moving_gk + column_part(dscore, query_rows)]
  transfers between devices with their start and end apart: 31 -> 0, of which waited for: 17 -> 0; matrix products, arithmetic and copies ran while one was open for 12% -> 0% of each run, Pallas kernels for 0% -> 0%
where the time goes in v1:
time: 105 us
  Pallas kernels  102 us (97%)
  local copies, waits for them, and re-layouts  1.62 us (2%)
    pallas_call x1, Pallas kernels, reduce(): pl.pallas_call(reduce_kernel, out_shape=jax.ShapeDtypeStruct((32, 1536),...  43.4 us
    pallas_call x1, Pallas kernels, spread(): pl.pallas_call(spread_kernel, out_shape=(blk(8), blk(8), blk(4), blk(4),...  22.5 us
    pallas_call x1, Pallas kernels, collect(): pl.pallas_call(collect_kernel, out_shape=jax.ShapeDtypeStruct((2, 3, 4, T...  17 us
    pallas_call x1, Pallas kernels, project(): pl.pallas_call(project_kernel, out_shape=(jax.ShapeDtypeStruct((6, 8, 8,...  9.95 us
    pallas_call x1, Pallas kernels, attention(): pl.pallas_call(attention_kernel, out_shape=(blk(4), blk(4), blk(8)), in_s...  9.33 us

profile of v1, /device:TPU:0, one launch (start us, length us, event | category | flops | bytes accessed | tf_op | source)
XLA Modules:
  0.0 104.5 jit_solution(10083192631678104544)
XLA Ops:
  0.6 22.5 %spread.1 = (bf16[8,256,128]{2,1,0:T(8,128)(2,1)}, bf16[8,256,128]{2,1,0:T(8,128)(2,1)}, bf16[4,256,128]{2,1,0:T(8,128)(2,1)}, bf16[4,256,128]{2,1,0:T(8,128)(2,...) custom-call(s32[1,16]{1,0:T(1,128)} %labels.1, s32[1,16]{1,0:T(1,128)} %layout.1, f32[1,4,256]{2,1,0:T(4,128)} %lse.1, ...), custom_call_target="tpu_custom_call" | custom-call | tf_op jit(solution)/shard_map/spread/pallas_call | solution.py:142
  23.2 9.3 %attention.1 = (bf16[4,256,128]{2,1,0:T(8,128)(2,1)}, bf16[4,256,128]{2,1,0:T(8,128)(2,1)}, bf16[8,256,128]{2,1,0:T(8,128)(2,1)}) custom-call(bf16[8,256,128]{2,1,0:T(8,128)(2,1)} %get-tuple-element.18.q, bf16[8,256,128]{2,1,0:T(8,128)(2,1)} %get-tuple-element.19.do, bf16[4,256,128]{2,1,0:T(8,128)(2,1)} %get-tuple-element.20.k, ...), custom_call_target="tpu_custom_call" | custom-call | tf_op jit(solution)/shard_map/attention/pallas_call | solution.py:215
  32.5 17.0 %collect.1.g = bf16[2,3,4,256,128]{4,3,2,1,0:T(8,128)(2,1)} custom-call(bf16[4,256,128]{2,1,0:T(8,128)(2,1)} %get-tuple-element.23.dk, bf16[4,256,128]{2,1,0:T(8,128)(2,1)} %get-tuple-element.24.dv, bf16[8,256,128]{2,1,0:T(8,128)(2,1)} %get-tuple-element.25.dq.dq_v, bf16[8,256,128]{2,1,0:T(8,128)(2,1)} %get-tuple-element.25.dq.dq_v), custom_call_target="tpu_custom_call" | custom-call | tf_op jit(solution)/shard_map/collect/pallas_call | solution.py:274
  49.5 9.9 %project.1 = (bf16[6,8,8,32,256]{4,3,2,1,0:T(8,128)(2,1)}, bf16[1,256,512]{2,1,0:T(8,128)(2,1)}, bf16[1,256,512]{2,1,0:T(8,128)(2,1)}, bf16[1,256,512]{2,1,0:T(8,128)(2,1)}) custom-call(s32[1]{0:T(128)} %bitcast.core, bf16[1,256,4096]{2,1,0:T(8,128)(2,1)} %xa.1, bf16[8,256,256]{2,1,0:T(8,128)(2,1)} %get-tuple-element.17.xb, ...), custom_call_target="tpu_custom_call" | custom-call | tf_op jit(solution)/shard_map/project/pallas_call | solution.py:314
  59.5 43.4 %reduce.1 = f32[32,1536]{1,0:T(8,128)} custom-call(bf16[6,2,4,4,2,32,256]{6,5,4,3,2,1,0:T(8,128)(2,1)} %bitcast.2), custom_call_target="tpu_custom_call" | custom-call | tf_op jit(solution)/shard_map/reduce/pallas_call | solution.py:446
  102.9 1.6 %copy.14 = f32[32,1536]{1,0:T(8,128)} copy(f32[32,1536]{1,0:T(8,128)} %reduce.1) | data formatting | bytes 393216

commit v2 on v0

v2 whole, which is shorter than its diff:
```python
import functools
import math

import jax
import jax.numpy as jnp
from jax import lax
from jax.experimental import pallas as pl
from jax.experimental.pallas import tpu as pltpu
from jax.sharding import PartitionSpec as P

HEADS = 4
HD = 128
TOK = 256
LOG2E = math.log2(math.e)
SCALE = 1.0 / math.sqrt(HD)
HIDDEN = 1e30
MESH = pl.DeviceIdType.MESH
F32 = jnp.float32
BF16 = jnp.bfloat16
ANY = pl.BlockSpec(memory_space=pl.ANY)
VM = pl.BlockSpec(memory_space=pltpu.VMEM)
SM = pl.BlockSpec(memory_space=pltpu.SMEM)


def place():
    dp = lax.axis_index("dp")
    ctx = lax.axis_index("ctx")
    core = lax.rem(dp, 2)
    x = lax.rem(dp // 2, 4)
    z_lo = dp // 8
    y = ctx // 2
    z_hi = lax.rem(ctx, 2)
    return core, x, y, z_lo, z_hi, dp, ctx


def flip(a, b):
    return lax.rem(a + b, 2)


def target(h):
    core, x, y, z_lo, z_hi, dp, ctx = place()
    return (dp - core + flip(1 + z_hi, y), h * 2 + flip(core, h))


def owner(s):
    core, x, y, z_lo, z_hi, dp, ctx = place()
    return (dp - core + flip(z_hi, y), s * 2 + flip(1 + core, s))


def greet(devices):
    barrier = pltpu.get_barrier_semaphore()
    for d in devices:
        pl.semaphore_signal(barrier, inc=1, device_id=d, device_id_type=MESH)
    return lambda: pl.semaphore_wait(barrier, len(devices))


def remote(src, dst, send, recv, device):
    return pltpu.make_async_remote_copy(
        src_ref=src, dst_ref=dst, send_sem=send, recv_sem=recv,
        device_id=device, device_id_type=MESH,
    )


def tile_rows(labels, layout, ctx):
    n0 = jnp.int32(0)
    n1 = jnp.int32(0)
    for j in range(16):
        lab = labels[0, j]
        n0 = n0 + jnp.where(lab == 0, 1, 0)
        n1 = n1 + jnp.where(lab == 1, 1, 0)
    n2 = 16 - n0 - n1
    out = []
    for t in range(2):
        lab = labels[0, layout[0, 2 * ctx + t]]
        own = jnp.where(lab == 1, n1, jnp.where(lab == 2, n2, 0))
        count = ((n0 + own) * 128).astype(F32)
        out.append((lab, jnp.log(jnp.full((1, 128), count, F32))))
    return out


def dot_t(a, b):
    return lax.dot_general(a, b, (((1,), (1,)), ((), ())), preferred_element_type=F32)


def dot_n(a, b):
    return lax.dot_general(a, b, (((1,), (0,)), ((), ())), preferred_element_type=F32)


def dot_l(a, b):
    return lax.dot_general(a, b, (((0,), (0,)), ((), ())), preferred_element_type=F32)


ORDERS = ("xyz", "yzx", "zxy")
SIZES = {"l": 2, "x": 4, "y": 4, "h": 2}


def left_over(dims, axis):
    return "".join(d for d in dims if d not in ("lh" if axis == "z" else axis))


def block(dims, axis, coord):
    want = {"l": lax.rem(coord, 2), "h": coord // 2} if axis == "z" else {axis: coord}
    return tuple(want.get(d, slice(None)) for d in dims)


class Job:
    def __init__(self, n, j, part, refs, sems, here, device):
        self.chunk = 2 * n + j
        self.part = part.at[self.chunk]
        self.got1, self.comb, self.tot1, self.got2, self.tot2, self.got3 = refs
        self.send, self.recv = sems
        self.axes = ORDERS[n]
        self.dims = ["lxyh"]
        for axis in self.axes:
            self.dims.append(left_over(self.dims[-1], axis))
        self.at = [here[a] for a in self.axes]
        self.device = lambda stage, by: device(self.axes[stage], by)
        self.sent = []

    def go(self, sem, src, dst, device):
        c = remote(src, dst, self.send.at[sem], self.recv.at[sem], device)
        c.start()
        self.sent.append(c)

    def await_(self, sem, dst):
        remote(dst, dst, self.send.at[sem], self.recv.at[sem], self.device(0, 1)).wait_recv()

    def piece1(self, half, by):
        idx = block("lxyh", self.axes[0], lax.rem(self.at[0] + by, 4))
        return self.part.at[(half,) + idx]

    def start1(self):
        right, left = self.device(0, 1), self.device(0, -1)
        self.go(0, self.piece1(0, 2), self.got1.at[0], right)
        self.go(1, self.piece1(1, 2), self.got1.at[1], left)
        self.go(2, self.piece1(1, 1), self.got1.at[2], right)
        self.go(3, self.piece1(0, 3), self.got1.at[3], left)

    def combine(self):
        for m, by in ((0, 1), (1, 3)):
            self.await_(m, self.got1.at[m])
            mine = self.piece1(m, by)[...]
            self.comb[m] = (self.got1[m].astype(F32) + mine.astype(F32)).astype(BF16)
            self.go(4 + m, self.comb.at[m], self.got1.at[4 + m], self.device(0, 1 if m == 0 else -1))

    def finish1(self):
        for half, raw in ((0, 3), (1, 2)):
            self.await_(raw, self.got1.at[raw])
            self.await_(4 + half, self.got1.at[4 + half])
            total = self.piece1(half, 0)[...].astype(F32)
            total += self.got1[raw].astype(F32) + self.got1[4 + half].astype(F32)
            self.tot1[half] = total.astype(BF16)
        self.direct(1, self.tot1, self.got2, 6)

    def piece(self, stage, ref, by):
        idx = block(self.dims[stage], self.axes[stage], lax.rem(self.at[stage] + by, 4))
        return ref.at[(slice(None),) + idx]

    def direct(self, stage, ref, got, sem):
        for by in (2, 1, 3):
            self.go(sem + by - 1, self.piece(stage, ref, by), got.at[by - 1], self.device(stage, by))

    def summed(self, stage, ref, got, sem):
        total = self.piece(stage, ref, 0)[...].astype(F32)
        for by in (1, 3, 2):
            self.await_(sem + by - 1, got.at[by - 1])
            total += got[by - 1].astype(F32)
        return total

    def finish2(self):
        self.tot2[...] = self.summed(1, self.tot1, self.got2, 6).astype(BF16)
        self.direct(2, self.tot2, self.got3, 9)

    def finish3(self, out):
        total = self.summed(2, self.tot2, self.got3, 9)
        for half in range(2):
            at = self.chunk * 256 + half * 128
            out[:, at : at + 128] = total[half]

    def drain(self):
        for c in self.sent:
            c.wait_send()


def solve_kernel(
    labels, layout, lse, do_v, o_v, x_v, q, k, v, do,
    g_out, w_out,
    aux, lab8, labo, xt, xother, ko, vo, qo, doo, auxo, dk_acc, dv_acc, p_s, ds_s,
    dk_b, dv_b, dq_own, dq_give, dq_got, dq_sum, g, part,
    send, recv, fsend, frecv, xsem, dsend, drecv, osend, orecv, gsend, grecv, rsend, rrecv,
    *bufs,
):
    core, x, y, z_lo, z_hi, dp, ctx = place()
    here = {"x": x, "y": y, "z": z_hi * 2 + z_lo}
    sibling = (dp + 1 - 2 * core, ctx)

    def device(axis, by):
        c = dict(here)
        c[axis] = lax.rem(c[axis] + by + 4, 4)
        return (lax.rem(c["z"], 2) * 8 + c["x"] * 2 + core, c["y"] * 2 + c["z"] // 2)

    ready = greet(
        [target(h) for h in range(4)]
        + [owner(s) for s in range(4)]
        + [sibling]
        + [device(a, by) for a in "xyz" for by in (1, 2, 3)]
    )

    tiles = tile_rows(labels, layout, ctx)
    labs = jnp.concatenate(
        [jnp.full((1, 128), lab, jnp.int32) for lab, _ in tiles], axis=1
    )
    logs = jnp.concatenate([lg for _, lg in tiles], axis=1)
    for h in range(HEADS):
        cols = slice(h * HD, (h + 1) * HD)
        prod = do_v[0, :, cols].astype(F32) * o_v[0, :, cols].astype(F32)
        delta = jnp.sum(prod.T, axis=0, keepdims=True)
        ln = (logs + lse[0, h : h + 1, :]) * LOG2E
        aux[h, 0:1, :] = ln
        aux[h, 1:2, :] = jnp.where(labs == 1, ln, HIDDEN)
        aux[h, 2:3, :] = jnp.where(labs == 2, ln, HIDDEN)
        aux[h, 3:4, :] = delta
        aux[h, 4:8, :] = jnp.zeros((4, TOK), F32)
    lab8[...] = jnp.broadcast_to(labs.astype(F32), (8, TOK))

    def turn(dst, which):
        def one(i, carry):
            at = pl.multiple_of((2 * i + which) * 256, 256)
            dst[i] = x_v[0, :, pl.ds(at, 256)].T
            return carry

        lax.fori_loop(0, 8, one, 0)

    turn(xother, 1 - core)
    dk_acc[...] = jnp.zeros_like(dk_acc)
    dv_acc[...] = jnp.zeros_like(dv_acc)
    ready()

    hops = (0, 1, 3, 2)
    arrays = ((k, ko), (v, vo), (q, qo), (do, doo), (aux, auxo), (lab8, labo))
    sends = []
    for group in ((5, 0, 1), (4, 2, 3)):
        for t in hops:
            h = lax.rem(y + t, 4)
            for n in group:
                src, dst = arrays[n]
                if n == 5:
                    piece = src
                elif n == 4:
                    piece = src.at[h]
                else:
                    piece = src.at[0, :, pl.ds(pl.multiple_of(h * HD, HD), HD)]
                c = remote(piece, dst.at[y], send.at[n, t], recv.at[n, y], target(h))
                c.start()
                sends.append(c)
    cross = remote(xother, xt.at[1], xsem.at[0], xsem.at[1], sibling)
    cross.start()
    turn(xt.at[0], core)

    def arrived(ref, sem):
        remote(ref, ref, send.at[0, 0], sem, sibling).wait_recv()

    def left(ref, sem):
        remote(ref, ref, sem, recv.at[0, 0], sibling).wait_send()

    def slot(i):
        return lax.rem(y + jnp.where(i == 0, 0, jnp.where(i == 1, 3, i - 1)), 4)

    for t in (0, 3, 1, 2):
        s = lax.rem(y + t, 4)
        for n in (5, 0, 1):
            arrived(arrays[n][1].at[s], recv.at[n, s])

    def attend(c):
        k_all = ko[...].reshape(4 * TOK, HD)
        v_all = vo[...].reshape(4 * TOK, HD)
        qc = qo[c]
        doc = doo[c]
        s = dot_t(k_all, qc)
        d = dot_t(v_all, doc)
        rows = auxo[c]
        delta = rows[3:4, :]
        for t in range(8):
            part_ = slice(t * 128, (t + 1) * 128)
            at = (t % 2) * 128
            lab = labo[t // 2, 0:1, at : at + 1]
            row = jnp.where(
                lab == 0.0, rows[0:1, :], jnp.where(lab == 1.0, rows[1:2, :], rows[2:3, :])
            )
            p = jnp.exp2(s[part_] * (SCALE * LOG2E) - row)
            p_s[part_, :] = p.astype(BF16)
            ds_s[part_, :] = (p * (d[part_] - delta) * SCALE).astype(BF16)
        p_b = p_s[...]
        ds_b = ds_s[...]
        dv_acc[...] += dot_n(p_b, doc)
        dk_acc[...] += dot_n(ds_b, qc)
        return dot_l(ds_b, k_all)

    def hand_over(i):
        s = slot(i)
        arrived(dq_got.at[s], drecv.at[s])
        dq_sum[s] = (dq_own[s] + dq_got[s].astype(F32)).astype(BF16)
        remote(dq_sum.at[s], g.at[0, 0, y], osend.at[0, s], orecv.at[0, y], owner(s)).start()

    def step(i, carry):
        s = slot(i)
        for n in (4, 2, 3):
            dst = arrays[n][1]
            arrived(dst.at[s], recv.at[n, s])
            remote(dst.at[s], dst.at[4 + s], fsend.at[n - 2, s], frecv.at[n - 2, s], sibling).start()
        dq_own[s] = attend(s)

        @pl.when(i > 0)
        def _():
            hand_over(i - 1)

        for n in (4, 2, 3):
            arrived(arrays[n][1].at[4 + s], frecv.at[n - 2, s])
        dq_give[s] = attend(4 + s).astype(BF16)
        remote(dq_give.at[s], dq_got.at[s], dsend.at[s], drecv.at[s], sibling).start()
        return carry

    lax.fori_loop(0, 4, step, 0)
    for n, acc, buf in ((2, dv_acc, dv_b), (1, dk_acc, dk_b)):
        buf[...] = acc[...].astype(BF16).reshape(4, TOK, HD)
        for t in (2, 1, 3, 0):
            s = lax.rem(y + t, 4)
            remote(buf.at[s], g.at[0, n, y], osend.at[n, s], orecv.at[n, y], owner(s)).start()
    hand_over(3)

    def relay(n):
        for t in (0, 1, 3, 2):
            h = lax.rem(y + t, 4)
            arrived(g.at[0, n, h], orecv.at[n, h])
            remote(g.at[0, n, h], g.at[1, n, h], gsend.at[n, h], grecv.at[n, h], sibling).start()

    def whole(n):
        for h in range(4):
            arrived(g.at[1, n, h], grecv.at[n, h])

    jobs = {}
    for n in range(3):
        for j in range(2):
            c = 2 * n + j
            jobs[n, j] = Job(
                n, j, part, bufs[6 * c : 6 * c + 6], (rsend.at[c], rrecv.at[c]), here, device
            )

    def gemm(n, j):
        rhs = jnp.concatenate(
            [jnp.concatenate([g[c, n, 2 * j], g[c, n, 2 * j + 1]], axis=1) for c in range(2)], axis=0
        )

        def rows(i, carry):
            lhs = jnp.concatenate([xt[0, i], xt[1, i]], axis=1)
            res = dot_n(lhs, rhs).astype(BF16)
            for half in range(2):
                part[2 * n + j, half, i // 4, lax.rem(i, 4)] = res[
                    :, half * 128 : (half + 1) * 128
                ].reshape(4, 2, 32, 128)
            return carry

        lax.fori_loop(0, 8, rows, 0)

    cross.wait()
    order = (2, 1, 0)
    relay(2)
    relay(1)
    whole(2)
    gemm(2, 0)
    jobs[2, 0].start1()
    relay(0)
    whole(1)
    gemm(1, 0)
    jobs[1, 0].start1()
    whole(0)
    gemm(0, 0)
    jobs[0, 0].start1()
    for n in order:
        gemm(n, 1)
    for n in order:
        jobs[n, 0].combine()
        jobs[n, 1].start1()
    for n in order:
        jobs[n, 0].finish1()
    g_out[...] = g[0]
    for n in order:
        jobs[n, 1].combine()
    for n in order:
        jobs[n, 0].finish2()
    for n in order:
        jobs[n, 1].finish1()
    for n in order:
        jobs[n, 0].finish3(w_out)
    for n in order:
        jobs[n, 1].finish2()
    for n in order:
        jobs[n, 1].finish3(w_out)

    for job in jobs.values():
        job.drain()
    for c in sends:
        c.wait_send()
    for s in range(4):
        for n in (2, 3, 4):
            left(arrays[n][1].at[s], fsend.at[n - 2, s])
        left(dq_give.at[s], dsend.at[s])
        for n in range(3):
            left(dq_sum.at[s], osend.at[n, s])
            left(g.at[0, n, s], gsend.at[n, s])


def solve(labels, layout, lse, q, k, v, o, do, x_in):
    blk = lambda *n: pltpu.VMEM((*n, TOK, HD), BF16)
    sem = lambda *n: pltpu.SemaphoreType.DMA(n)
    scratch = [
        pltpu.VMEM((4, 8, TOK), F32),
        pltpu.VMEM((8, TOK), F32),
        pltpu.VMEM((4, 8, TOK), F32),
        pltpu.VMEM((2, 8, 256, TOK), BF16),
        pltpu.VMEM((8, 256, TOK), BF16),
        blk(4), blk(4), blk(8), blk(8),
        pltpu.VMEM((8, 8, TOK), F32),
        pltpu.VMEM((1024, HD), F32),
        pltpu.VMEM((1024, HD), F32),
        pltpu.VMEM((1024, TOK), BF16),
        pltpu.VMEM((1024, TOK), BF16),
        blk(4), blk(4),
        pltpu.VMEM((4, TOK, HD), F32),
        blk(4), blk(4), blk(4),
        blk(2, 3, 4),
        pltpu.VMEM((6, 2, 2, 4, 4, 2, 32, 128), BF16),
        sem(6, 4), sem(6, 4), sem(3, 4), sem(3, 4), sem(2), sem(4), sem(4),
        sem(3, 4), sem(3, 4), sem(3, 4), sem(3, 4), sem(6, 12), sem(6, 12),
    ]
    for n in range(3):
        for j in range(2):
            dims = ["lxyh"]
            for axis in ORDERS[n]:
                dims.append(left_over(dims[-1], axis))
            s1, s2, s3 = [tuple(SIZES[d] for d in ds) + (32, 128) for ds in dims[1:]]
            for shape in ((6,) + s1, (2,) + s1, (2,) + s1, (3, 2) + s2, (2,) + s2, (3, 2) + s3):
                scratch.append(pltpu.VMEM(shape, BF16))
    return pl.pallas_call(
        solve_kernel,
        out_shape=(
            jax.ShapeDtypeStruct((3, 4, TOK, HD), BF16),
            jax.ShapeDtypeStruct((32, 1536), F32),
        ),
        in_specs=[SM, SM, VM, VM, VM, VM, ANY, ANY, ANY, ANY],
        out_specs=(VM, VM),
        scratch_shapes=scratch,
        compiler_params=pltpu.CompilerParams(collective_id=0, has_side_effects=True),
        name="solve",
    )(labels, layout, lse, do, o, x_in, q, k, v, do)


def finish_kernel(g, w, gq, gk, gv, gw):
    for t, out in enumerate((gq, gk, gv)):
        for h in range(4):
            out[0, :, h * HD : (h + 1) * HD] = g[t, h]
    gw[...] = w[...]


def finish(g, w):
    grad = jax.ShapeDtypeStruct((1, TOK, HEADS * HD), BF16)
    return pl.pallas_call(
        finish_kernel,
        out_shape=(grad, grad, grad, jax.ShapeDtypeStruct(w.shape, w.dtype)),
        in_specs=[VM, VM],
        out_specs=(VM,) * 4,
        name="finish",
    )(g, w)


def per_device(inputs, queries, keys, values, attn_out, grad_out, lse_shift, labels, layout):
    g, w = solve(labels, layout, lse_shift, queries, keys, values, attn_out, grad_out, inputs)
    return finish(g, w)


def solution(mesh):
    tok = P("dp", "ctx", None)
    return jax.shard_map(
        per_device,
        mesh=mesh,
        in_specs=(tok,) * 6 + (P("dp", None, "ctx"), P("dp", None), P("dp", None)),
        out_specs=(tok, tok, tok, P(("dp", "ctx"), None)),
        check_vma=False,
    )
```

time: 1100 us -> 85.3 us (0.08)
  waiting for transfers between devices: 880 us -> 0 us
  Pallas kernels: 0 us -> 84.1 us
  local copies, waits for them, and re-layouts: 69.7 us -> 0 us
  matrix products: 55.7 us -> 0 us
  other arithmetic: 44.7 us -> 0 us
  starting transfers between devices: 33.3 us -> 0 us
  between operations: 14.5 us -> 0.64 us
    unnamed x2 -> x0, waiting for transfers between devices: 716 us -> none
    ppermute x30 -> x0, waiting for transfers between devices: 164 us -> none  [shifted(): lax.ppermute(array, axis, [(i, (i + by) % peers) for i in range(peers)])]
    pallas_call x0 -> x2, Pallas kernels: none -> 84.1 us  [the longest x1 81.9 us: solve(): pl.pallas_call(solve_kernel, out_shape=(jax.ShapeDtypeStruct((3, 4, TOK,...]
    dot_general x41 -> x0, matrix products: 55.7 us -> none  [the longest x16 15.4 us: column_part(): jnp.einsum('hqk,qhd->khd', matrix, split_heads(query_rows), preferred_ele...]
    unnamed x53 -> x0, local copies, waits for them, and re-layouts: 33.9 us -> none
    ppermute x30 -> x0, starting transfers between devices: 33.3 us -> none  [shifted(): lax.ppermute(array, axis, [(i, (i + by) % peers) for i in range(peers)])]
    reshape x16 -> x0, local copies, waits for them, and re-layouts: 29.7 us -> none  [column_part(): return result.reshape(matrix.shape[2], HEADS * HEAD_DIM)]
    add x16 -> x0, other arithmetic: 28.7 us -> none  [the longest x7 14.2 us: per_device(): moving_gk = moving_gk + column_part(dscore, query_rows)]
  transfers between devices with their start and end apart: 31 -> 0, of which waited for: 17 -> 0; matrix products, arithmetic and copies ran while one was open for 12% -> 0% of each run, Pallas kernels for 0% -> 0%
where the time goes in v2:
time: 85.3 us; the launch traced here: 84.8 us
  Pallas kernels  84.1 us (99%)
    pallas_call x1, Pallas kernels, solve(): pl.pallas_call(solve_kernel, out_shape=(jax.ShapeDtypeStruct((3, 4, TOK,...  81.9 us
    pallas_call x1, Pallas kernels, finish(): pl.pallas_call(finish_kernel, out_shape=(grad, grad, grad, jax.ShapeDtype...  2.24 us

profile of v2, /device:TPU:0, one launch (start us, length us, event | category | flops | bytes accessed | tf_op | source)
XLA Modules:
  0.0 84.8 jit_solution(18150767064730880259)
XLA Ops:
  0.6 81.9 %solve.1 = (bf16[3,4,256,128]{3,2,1,0:T(8,128)(2,1)}, f32[32,1536]{1,0:T(8,128)}) custom-call(s32[1,16]{1,0:T(1,128)} %labels.1, s32[1,16]{1,0:T(1,128)} %layout.1, f32[1,4,256]{2,1,0:T(4,128)} %lse.1, bf16[1,256,512]{2,1,0:T(8,128)(2,1)} %do.1, bf16[1,256,512]{2,1,0:T(8,128)(2,1)} %o_v.1, bf16[1,256,4096]{2,1,0:T(8,128)(2,1)} %x_v.1, ...), custom_call_target="tpu_custom_call" | custom-call | tf_op jit(solution)/shard_map/solve/pallas_call | solution.py:444
  82.5 2.2 %finish.1 = (bf16[1,256,512]{2,1,0:T(8,128)(2,1)}, bf16[1,256,512]{2,1,0:T(8,128)(2,1)}, bf16[1,256,512]{2,1,0:T(8,128)(2,1)}, f32[32,1536]{1,0:T(8,128)}) custom-call(bf16[3,4,256,128]{3,2,1,0:T(8,128)(2,1)} %get-tuple-element.6.g, f32[32,1536]{1,0:T(8,128)} %get-tuple-element.7.w), custom_call_target="tpu_custom_call" | custom-call | tf_op jit(solution)/shard_map/finish/pallas_call | solution.py:467

commit v3 on v2

--- a/solution.py
+++ b/solution.py
@@ -90,7 +90,7 @@
     return lax.dot_general(a, b, (((0,), (0,)), ((), ())), preferred_element_type=F32)
 
 
-ORDERS = ("xyz", "yzx", "zxy")
+ORDERS = ("zxy", "yzx", "xyz")
 SIZES = {"l": 2, "x": 4, "y": 4, "h": 2}
 
 
@@ -183,10 +183,11 @@
 
 
 def solve_kernel(
-    labels, layout, lse, do_v, o_v, x_v, q, k, v, do,
+    labels_hbm, layout_hbm, lse_hbm, x_hbm, o, q, k, v, do,
     g_out, w_out,
-    aux, lab8, labo, xt, xother, ko, vo, qo, doo, auxo, dk_acc, dv_acc, p_s, ds_s,
-    dk_b, dv_b, dq_own, dq_give, dq_got, dq_sum, g, part,
+    labels, layout, lse, do_v, o_v, x_v, load,
+    aux, lab8, labo, xt, xother, ko, vo, qo, doo, auxo, dq_acc, p_s, ds_s,
+    dk_b, dv_b, dq_give, dq_got, dq_sum, g, part,
     send, recv, fsend, frecv, xsem, dsend, drecv, osend, orecv, gsend, grecv, rsend, rrecv,
     *bufs,
 ):
@@ -206,6 +207,38 @@
         + [device(a, by) for a in "xyz" for by in (1, 2, 3)]
     )
 
+    loads = [
+        pltpu.make_async_copy(src, dst, load.at[i])
+        for i, (src, dst) in enumerate(
+            ((labels_hbm, labels), (layout_hbm, layout), (lse_hbm, lse), (do, do_v), (o, o_v), (x_hbm, x_v))
+        )
+    ]
+    for c in loads:
+        c.start()
+    ready()
+
+    hops = (2, 1, 3, 0)
+    arrays = ((k, ko), (v, vo), (q, qo), (do, doo), (aux, auxo), (lab8, labo))
+    sends = []
+
+    def give(n, t):
+        h = lax.rem(y + t, 4)
+        src, dst = arrays[n]
+        if n == 5:
+            piece = src
+        elif n == 4:
+            piece = src.at[h]
+        else:
+            piece = src.at[0, :, pl.ds(pl.multiple_of(h * HD, HD), HD)]
+        c = remote(piece, dst.at[y], send.at[n, t], recv.at[n, y], target(h))
+        c.start()
+        sends.append(c)
+
+    for t in hops:
+        give(2, t)
+        give(3, t)
+    for c in loads[:5]:
+        c.wait()
     tiles = tile_rows(labels, layout, ctx)
     labs = jnp.concatenate(
         [jnp.full((1, 128), lab, jnp.int32) for lab, _ in tiles], axis=1
@@ -223,6 +256,13 @@
         aux[h, 4:8, :] = jnp.zeros((4, TOK), F32)
     lab8[...] = jnp.broadcast_to(labs.astype(F32), (8, TOK))
 
+    for t in hops:
+        give(4, t)
+    for t in hops:
+        give(5, t)
+        give(0, t)
+        give(1, t)
+
     def turn(dst, which):
         def one(i, carry):
             at = pl.multiple_of((2 * i + which) * 256, 256)
@@ -231,31 +271,12 @@
 
         lax.fori_loop(0, 8, one, 0)
 
+    loads[5].wait()
     turn(xother, 1 - core)
-    dk_acc[...] = jnp.zeros_like(dk_acc)
-    dv_acc[...] = jnp.zeros_like(dv_acc)
-    ready()
-
-    hops = (0, 1, 3, 2)
-    arrays = ((k, ko), (v, vo), (q, qo), (do, doo), (aux, auxo), (lab8, labo))
-    sends = []
-    for group in ((5, 0, 1), (4, 2, 3)):
-        for t in hops:
-            h = lax.rem(y + t, 4)
-            for n in group:
-                src, dst = arrays[n]
-                if n == 5:
-                    piece = src
-                elif n == 4:
-                    piece = src.at[h]
-                else:
-                    piece = src.at[0, :, pl.ds(pl.multiple_of(h * HD, HD), HD)]
-                c = remote(piece, dst.at[y], send.at[n, t], recv.at[n, y], target(h))
-                c.start()
-                sends.append(c)
     cross = remote(xother, xt.at[1], xsem.at[0], xsem.at[1], sibling)
     cross.start()
     turn(xt.at[0], core)
+    dq_acc[...] = jnp.zeros_like(dq_acc)
 
     def arrived(ref, sem):
         remote(ref, ref, send.at[0, 0], sem, sibling).wait_recv()
@@ -264,72 +285,64 @@
         remote(ref, ref, sem, recv.at[0, 0], sibling).wait_send()
 
     def slot(i):
-        return lax.rem(y + jnp.where(i == 0, 0, jnp.where(i == 1, 3, i - 1)), 4)
-
-    for t in (0, 3, 1, 2):
+        return lax.rem(y + jnp.where(i == 0, 2, jnp.where(i == 1, 3, 3 - i)), 4)
+
+    near = (2, 3, 1, 0)
+    for t in near:
         s = lax.rem(y + t, 4)
-        for n in (5, 0, 1):
-            arrived(arrays[n][1].at[s], recv.at[n, s])
-
-    def attend(c):
-        k_all = ko[...].reshape(4 * TOK, HD)
-        v_all = vo[...].reshape(4 * TOK, HD)
-        qc = qo[c]
-        doc = doo[c]
-        s = dot_t(k_all, qc)
-        d = dot_t(v_all, doc)
-        rows = auxo[c]
-        delta = rows[3:4, :]
-        for t in range(8):
-            part_ = slice(t * 128, (t + 1) * 128)
-            at = (t % 2) * 128
-            lab = labo[t // 2, 0:1, at : at + 1]
-            row = jnp.where(
-                lab == 0.0, rows[0:1, :], jnp.where(lab == 1.0, rows[1:2, :], rows[2:3, :])
-            )
-            p = jnp.exp2(s[part_] * (SCALE * LOG2E) - row)
-            p_s[part_, :] = p.astype(BF16)
-            ds_s[part_, :] = (p * (d[part_] - delta) * SCALE).astype(BF16)
-        p_b = p_s[...]
-        ds_b = ds_s[...]
-        dv_acc[...] += dot_n(p_b, doc)
-        dk_acc[...] += dot_n(ds_b, qc)
-        return dot_l(ds_b, k_all)
-
-    def hand_over(i):
-        s = slot(i)
-        arrived(dq_got.at[s], drecv.at[s])
-        dq_sum[s] = (dq_own[s] + dq_got[s].astype(F32)).astype(BF16)
-        remote(dq_sum.at[s], g.at[0, 0, y], osend.at[0, s], orecv.at[0, y], owner(s)).start()
-
-    def step(i, carry):
-        s = slot(i)
-        for n in (4, 2, 3):
+        for n in (2, 3, 4):
             dst = arrays[n][1]
             arrived(dst.at[s], recv.at[n, s])
             remote(dst.at[s], dst.at[4 + s], fsend.at[n - 2, s], frecv.at[n - 2, s], sibling).start()
-        dq_own[s] = attend(s)
-
-        @pl.when(i > 0)
-        def _():
-            hand_over(i - 1)
-
-        for n in (4, 2, 3):
+    for t in near:
+        s = lax.rem(y + t, 4)
+        for n in (2, 3, 4):
             arrived(arrays[n][1].at[4 + s], frecv.at[n - 2, s])
-        dq_give[s] = attend(4 + s).astype(BF16)
+
+    def keys(i, carry):
+        s = slot(i)
+        for n in (5, 0, 1):
+            arrived(arrays[n][1].at[s], recv.at[n, s])
+        k_b = ko[s]
+        v_b = vo[s]
+        for c in range(4):
+            pair = slice(2 * c, 2 * c + 2)
+            sc = dot_t(k_b, qo[pair].reshape(2 * TOK, HD))
+            dp_ = dot_t(v_b, doo[pair].reshape(2 * TOK, HD))
+            rows = jnp.concatenate([auxo[2 * c], auxo[2 * c + 1]], axis=1)
+            delta = rows[3:4, :]
+            cols = slice(c * 2 * TOK, (c + 1) * 2 * TOK)
+            for t in range(2):
+                part_ = slice(t * 128, (t + 1) * 128)
+                lab = labo[s, 0:1, t * 128 : t * 128 + 1]
+                row = jnp.where(
+                    lab == 0.0, rows[0:1, :], jnp.where(lab == 1.0, rows[1:2, :], rows[2:3, :])
+                )
+                p = jnp.exp2(sc[part_] * (SCALE * LOG2E) - row)
+                p_s[part_, cols] = p.astype(BF16)
+                ds_s[part_, cols] = (p * (dp_[part_] - delta) * SCALE).astype(BF16)
+        q_all = qo[...].reshape(8 * TOK, HD)
+        do_all = doo[...].reshape(8 * TOK, HD)
+        dv_b[s] = dot_n(p_s[...], do_all).astype(BF16)
+        remote(dv_b.at[s], g.at[0, 2, y], osend.at[2, s], orecv.at[2, y], owner(s)).start()
+        dk_b[s] = dot_n(ds_s[...], q_all).astype(BF16)
+        remote(dk_b.at[s], g.at[0, 1, y], osend.at[1, s], orecv.at[1, y], owner(s)).start()
+        dq_acc[...] += dot_l(ds_s[...], k_b).reshape(8, TOK, HD)
+        return carry
+
+    lax.fori_loop(0, 4, keys, 0)
+    for t in (2, 3, 1, 0):
+        s = lax.rem(y + t, 4)
+        dq_give[s] = dq_acc[4 + s].astype(BF16)
         remote(dq_give.at[s], dq_got.at[s], dsend.at[s], drecv.at[s], sibling).start()
-        return carry
-
-    lax.fori_loop(0, 4, step, 0)
-    for n, acc, buf in ((2, dv_acc, dv_b), (1, dk_acc, dk_b)):
-        buf[...] = acc[...].astype(BF16).reshape(4, TOK, HD)
-        for t in (2, 1, 3, 0):
-            s = lax.rem(y + t, 4)
-            remote(buf.at[s], g.at[0, n, y], osend.at[n, s], orecv.at[n, y], owner(s)).start()
-    hand_over(3)
-
-    def relay(n):
-        for t in (0, 1, 3, 2):
+    for t in (2, 3, 1, 0):
+        s = lax.rem(y + t, 4)
+        arrived(dq_got.at[s], drecv.at[s])
+        dq_sum[s] = (dq_acc[s] + dq_got[s].astype(F32)).astype(BF16)
+        remote(dq_sum.at[s], g.at[0, 0, y], osend.at[0, s], orecv.at[0, y], owner(s)).start()
+
+    def relay(*parts):
+        for t, n in ((t, n) for t in (2, 1, 3, 0) for n in parts):
             h = lax.rem(y + t, 4)
             arrived(g.at[0, n, h], orecv.at[n, h])
             remote(g.at[0, n, h], g.at[1, n, h], gsend.at[n, h], grecv.at[n, h], sibling).start()
@@ -352,20 +365,21 @@
         )
 
         def rows(i, carry):
-            lhs = jnp.concatenate([xt[0, i], xt[1, i]], axis=1)
+            lhs = jnp.concatenate(
+                [xt[c, pl.ds(i * 4, 4)].reshape(1024, TOK) for c in range(2)], axis=1
+            )
             res = dot_n(lhs, rhs).astype(BF16)
             for half in range(2):
-                part[2 * n + j, half, i // 4, lax.rem(i, 4)] = res[
-                    :, half * 128 : (half + 1) * 128
-                ].reshape(4, 2, 32, 128)
+                part[2 * n + j, half, i] = res[:, half * 128 : (half + 1) * 128].reshape(
+                    4, 4, 2, 32, 128
+                )
             return carry
 
-        lax.fori_loop(0, 8, rows, 0)
+        lax.fori_loop(0, 2, rows, 0)
 
     cross.wait()
     order = (2, 1, 0)
-    relay(2)
-    relay(1)
+    relay(2, 1)
     whole(2)
     gemm(2, 0)
     jobs[2, 0].start1()
@@ -414,6 +428,13 @@
     blk = lambda *n: pltpu.VMEM((*n, TOK, HD), BF16)
     sem = lambda *n: pltpu.SemaphoreType.DMA(n)
     scratch = [
+        pltpu.SMEM((1, 16), jnp.int32),
+        pltpu.SMEM((1, 16), jnp.int32),
+        pltpu.VMEM((1, 4, TOK), F32),
+        pltpu.VMEM((1, TOK, 512), BF16),
+        pltpu.VMEM((1, TOK, 512), BF16),
+        pltpu.VMEM((1, TOK, 4096), BF16),
+        sem(6),
         pltpu.VMEM((4, 8, TOK), F32),
         pltpu.VMEM((8, TOK), F32),
         pltpu.VMEM((4, 8, TOK), F32),
@@ -421,12 +442,10 @@
         pltpu.VMEM((8, 256, TOK), BF16),
         blk(4), blk(4), blk(8), blk(8),
         pltpu.VMEM((8, 8, TOK), F32),
-        pltpu.VMEM((1024, HD), F32),
-        pltpu.VMEM((1024, HD), F32),
-        pltpu.VMEM((1024, TOK), BF16),
-        pltpu.VMEM((1024, TOK), BF16),
+        pltpu.VMEM((8, TOK, HD), F32),
+        pltpu.VMEM((TOK, 2048), BF16),
+        pltpu.VMEM((TOK, 2048), BF16),
         blk(4), blk(4),
-        pltpu.VMEM((4, TOK, HD), F32),
         blk(4), blk(4), blk(4),
         blk(2, 3, 4),
         pltpu.VMEM((6, 2, 2, 4, 4, 2, 32, 128), BF16),
@@ -447,12 +466,12 @@
             jax.ShapeDtypeStruct((3, 4, TOK, HD), BF16),
             jax.ShapeDtypeStruct((32, 1536), F32),
         ),
-        in_specs=[SM, SM, VM, VM, VM, VM, ANY, ANY, ANY, ANY],
+        in_specs=[ANY] * 9,
         out_specs=(VM, VM),
         scratch_shapes=scratch,
         compiler_params=pltpu.CompilerParams(collective_id=0, has_side_effects=True),
         name="solve",
-    )(labels, layout, lse, do, o, x_in, q, k, v, do)
+    )(labels, layout, lse, x_in, o, q, k, v, do)
 
 
 def finish_kernel(g, w, gq, gk, gv, gw):

time: 85.3 us -> 75.5 us (0.89)
  Pallas kernels: 84.1 us -> 74.7 us
    pallas_call x1, Pallas kernels: 81.9 us -> 72.5 us  [solve(): pl.pallas_call(solve_kernel, out_shape=(jax.ShapeDtypeStruct((3, 4, TOK,...]
where the time goes in v3:
time: 75.5 us; the launch traced here: 75.4 us
  Pallas kernels  74.7 us (99%)
    pallas_call x1, Pallas kernels, solve(): pl.pallas_call(solve_kernel, out_shape=(jax.ShapeDtypeStruct((3, 4, TOK,...  72.5 us
    pallas_call x1, Pallas kernels, finish(): pl.pallas_call(finish_kernel, out_shape=(grad, grad, grad, jax.ShapeDtype...  2.24 us

profile of v3, /device:TPU:0, one launch (start us, length us, event | category | flops | bytes accessed | tf_op | source)
XLA Modules:
  0.0 75.4 jit_solution(3304233478962686880)
XLA Ops:
  0.6 72.5 %solve.1 = (bf16[3,4,256,128]{3,2,1,0:T(8,128)(2,1)}, f32[32,1536]{1,0:T(8,128)}) custom-call(s32[1,16]{1,0:T(1,128)} %labels_hbm.1, s32[1,16]{1,0:T(1,128)} %layout_hbm.1, f32[1,4,256]{2,1,0:T(4,128)} %lse_hbm.1, bf16[1,256,4096]{2,1,0:T(8,128)(2,1)} %x_hbm.1, bf16[1,256,512]{2,1,0:T(8,128)(2,1)} %o.1, bf16[1,256,512]{2,1,0:T(8,128)(2,1)} %q.1, ...), custom_call_target="tpu_custom_call" | custom-call | tf_op jit(solution)/shard_map/solve/pallas_call | solution.py:463
  73.1 2.2 %finish.1 = (bf16[1,256,512]{2,1,0:T(8,128)(2,1)}, bf16[1,256,512]{2,1,0:T(8,128)(2,1)}, bf16[1,256,512]{2,1,0:T(8,128)(2,1)}, f32[32,1536]{1,0:T(8,128)}) custom-call(bf16[3,4,256,128]{3,2,1,0:T(8,128)(2,1)} %get-tuple-element.6.g, f32[32,1536]{1,0:T(8,128)} %get-tuple-element.7.w), custom_call_target="tpu_custom_call" | custom-call | tf_op jit(solution)/shard_map/finish/pallas_call | solution.py:486

commit v4 on v3

--- a/solution.py
+++ b/solution.py
@@ -90,7 +90,8 @@
     return lax.dot_general(a, b, (((0,), (0,)), ((), ())), preferred_element_type=F32)
 
 
-ORDERS = ("zxy", "yzx", "xyz")
+ORDERS = ("xyz", "yzx", "zxy")
+CHUNKS = ((2, 0), (2, 1), (1, 0), (1, 1), (0, 0), (0, 1))
 SIZES = {"l": 2, "x": 4, "y": 4, "h": 2}
 
 
@@ -104,12 +105,12 @@
 
 
 class Job:
-    def __init__(self, n, j, part, refs, sems, here, device):
+    def __init__(self, n, j, axes, part, refs, sems, here, device):
         self.chunk = 2 * n + j
         self.part = part.at[self.chunk]
         self.got1, self.comb, self.tot1, self.got2, self.tot2, self.got3 = refs
         self.send, self.recv = sems
-        self.axes = ORDERS[n]
+        self.axes = axes
         self.dims = ["lxyh"]
         for axis in self.axes:
             self.dims.append(left_over(self.dims[-1], axis))
@@ -184,8 +185,8 @@
 
 def solve_kernel(
     labels_hbm, layout_hbm, lse_hbm, x_hbm, o, q, k, v, do,
-    g_out, w_out,
-    labels, layout, lse, do_v, o_v, x_v, load,
+    gq_out, gk_out, gv_out, w_out,
+    labels, layout, lse, do_v, o_v, x_v, load, gout,
     aux, lab8, labo, xt, xother, ko, vo, qo, doo, auxo, dq_acc, p_s, ds_s,
     dk_b, dv_b, dq_give, dq_got, dq_sum, g, part,
     send, recv, fsend, frecv, xsem, dsend, drecv, osend, orecv, gsend, grecv, rsend, rrecv,
@@ -217,7 +218,7 @@
         c.start()
     ready()
 
-    hops = (2, 1, 3, 0)
+    hops = (1, 3, 2, 0)
     arrays = ((k, ko), (v, vo), (q, qo), (do, doo), (aux, auxo), (lab8, labo))
     sends = []
 
@@ -285,9 +286,9 @@
         remote(ref, ref, sem, recv.at[0, 0], sibling).wait_send()
 
     def slot(i):
-        return lax.rem(y + jnp.where(i == 0, 2, jnp.where(i == 1, 3, 3 - i)), 4)
-
-    near = (2, 3, 1, 0)
+        return lax.rem(y + jnp.where(i == 0, 3, jnp.where(i == 3, 0, i)), 4)
+
+    near = (3, 1, 2, 0)
     for t in near:
         s = lax.rem(y + t, 4)
         for n in (2, 3, 4):
@@ -342,7 +343,7 @@
         remote(dq_sum.at[s], g.at[0, 0, y], osend.at[0, s], orecv.at[0, y], owner(s)).start()
 
     def relay(*parts):
-        for t, n in ((t, n) for t in (2, 1, 3, 0) for n in parts):
+        for t, n in ((t, n) for t in (1, 3, 2, 0) for n in parts):
             h = lax.rem(y + t, 4)
             arrived(g.at[0, n, h], orecv.at[n, h])
             remote(g.at[0, n, h], g.at[1, n, h], gsend.at[n, h], grecv.at[n, h], sibling).start()
@@ -351,13 +352,14 @@
         for h in range(4):
             arrived(g.at[1, n, h], grecv.at[n, h])
 
-    jobs = {}
-    for n in range(3):
-        for j in range(2):
-            c = 2 * n + j
-            jobs[n, j] = Job(
-                n, j, part, bufs[6 * c : 6 * c + 6], (rsend.at[c], rrecv.at[c]), here, device
+    jobs = []
+    for c, (n, j) in enumerate(CHUNKS):
+        jobs.append(
+            Job(
+                n, j, ORDERS[c % 3], part, bufs[6 * c : 6 * c + 6],
+                (rsend.at[c], rrecv.at[c]), here, device,
             )
+        )
 
     def gemm(n, j):
         rhs = jnp.concatenate(
@@ -378,41 +380,49 @@
         lax.fori_loop(0, 2, rows, 0)
 
     cross.wait()
-    order = (2, 1, 0)
+    first, second = jobs[:3], jobs[3:]
     relay(2, 1)
     whole(2)
-    gemm(2, 0)
-    jobs[2, 0].start1()
+    for c in range(2):
+        gemm(*CHUNKS[c])
+        first[c].start1()
+    whole(1)
+    gemm(*CHUNKS[2])
+    first[2].start1()
+    gemm(*CHUNKS[3])
     relay(0)
-    whole(1)
-    gemm(1, 0)
-    jobs[1, 0].start1()
     whole(0)
-    gemm(0, 0)
-    jobs[0, 0].start1()
-    for n in order:
-        gemm(n, 1)
-    for n in order:
-        jobs[n, 0].combine()
-        jobs[n, 1].start1()
-    for n in order:
-        jobs[n, 0].finish1()
-    g_out[...] = g[0]
-    for n in order:
-        jobs[n, 1].combine()
-    for n in order:
-        jobs[n, 0].finish2()
-    for n in order:
-        jobs[n, 1].finish1()
-    for n in order:
-        jobs[n, 0].finish3(w_out)
-    for n in order:
-        jobs[n, 1].finish2()
-    for n in order:
-        jobs[n, 1].finish3(w_out)
-
-    for job in jobs.values():
+    gemm(*CHUNKS[4])
+    gemm(*CHUNKS[5])
+    for one, two in zip(first, second):
+        one.combine()
+        two.start1()
+    for one in first:
+        one.finish1()
+    outs = [
+        pltpu.make_async_copy(g.at[0, n, h], dst.at[0, :, h * HD : (h + 1) * HD], gout.at[n, h])
+        for n, dst in enumerate((gq_out, gk_out, gv_out))
+        for h in range(HEADS)
+    ]
+    for c in outs:
+        c.start()
+    for two in second:
+        two.combine()
+    for one in first:
+        one.finish2()
+    for two in second:
+        two.finish1()
+    for one in first:
+        one.finish3(w_out)
+    for two in second:
+        two.finish2()
+    for two in second:
+        two.finish3(w_out)
+
+    for job in jobs:
         job.drain()
+    for c in outs:
+        c.wait()
     for c in sends:
         c.wait_send()
     for s in range(4):
@@ -435,6 +445,7 @@
         pltpu.VMEM((1, TOK, 512), BF16),
         pltpu.VMEM((1, TOK, 4096), BF16),
         sem(6),
+        sem(3, 4),
         pltpu.VMEM((4, 8, TOK), F32),
         pltpu.VMEM((8, TOK), F32),
         pltpu.VMEM((4, 8, TOK), F32),
@@ -452,49 +463,56 @@
         sem(6, 4), sem(6, 4), sem(3, 4), sem(3, 4), sem(2), sem(4), sem(4),
         sem(3, 4), sem(3, 4), sem(3, 4), sem(3, 4), sem(6, 12), sem(6, 12),
     ]
-    for n in range(3):
-        for j in range(2):
-            dims = ["lxyh"]
-            for axis in ORDERS[n]:
-                dims.append(left_over(dims[-1], axis))
-            s1, s2, s3 = [tuple(SIZES[d] for d in ds) + (32, 128) for ds in dims[1:]]
-            for shape in ((6,) + s1, (2,) + s1, (2,) + s1, (3, 2) + s2, (2,) + s2, (3, 2) + s3):
-                scratch.append(pltpu.VMEM(shape, BF16))
+    for c in range(6):
+        dims = ["lxyh"]
+        for axis in ORDERS[c % 3]:
+            dims.append(left_over(dims[-1], axis))
+        s1, s2, s3 = [tuple(SIZES[d] for d in ds) + (32, 128) for ds in dims[1:]]
+        for shape in ((6,) + s1, (2,) + s1, (2,) + s1, (3, 2) + s2, (2,) + s2, (3, 2) + s3):
+            scratch.append(pltpu.VMEM(shape, BF16))
     return pl.pallas_call(
         solve_kernel,
         out_shape=(
-            jax.ShapeDtypeStruct((3, 4, TOK, HD), BF16),
+            *(jax.ShapeDtypeStruct((1, TOK, HEADS * HD), BF16),) * 3,
             jax.ShapeDtypeStruct((32, 1536), F32),
         ),
         in_specs=[ANY] * 9,
-        out_specs=(VM, VM),
+        out_specs=(ANY, ANY, ANY, VM),
         scratch_shapes=scratch,
         compiler_params=pltpu.CompilerParams(collective_id=0, has_side_effects=True),
         name="solve",
     )(labels, layout, lse, x_in, o, q, k, v, do)
 
 
-def finish_kernel(g, w, gq, gk, gv, gw):
-    for t, out in enumerate((gq, gk, gv)):
-        for h in range(4):
-            out[0, :, h * HD : (h + 1) * HD] = g[t, h]
-    gw[...] = w[...]
-
-
-def finish(g, w):
-    grad = jax.ShapeDtypeStruct((1, TOK, HEADS * HD), BF16)
+def finish_kernel(*refs):
+    ins, outs, bufs = refs[:4], refs[4:8], refs[8:12]
+    got, put = refs[12:]
+    loads = [pltpu.make_async_copy(a, b, got.at[i]) for i, (a, b) in enumerate(zip(ins, bufs))]
+    stores = [pltpu.make_async_copy(a, b, put.at[i]) for i, (a, b) in enumerate(zip(bufs, outs))]
+    for c in loads:
+        c.start()
+    for a, b in zip(loads, stores):
+        a.wait()
+        b.start()
+    for c in stores:
+        c.wait()
+
+
+def finish(*arrays):
     return pl.pallas_call(
         finish_kernel,
-        out_shape=(grad, grad, grad, jax.ShapeDtypeStruct(w.shape, w.dtype)),
-        in_specs=[VM, VM],
-        out_specs=(VM,) * 4,
+        out_shape=tuple(jax.ShapeDtypeStruct(a.shape, a.dtype) for a in arrays),
+        in_specs=[ANY] * 4,
+        out_specs=(ANY,) * 4,
+        scratch_shapes=[pltpu.VMEM(a.shape, a.dtype) for a in arrays]
+        + [pltpu.SemaphoreType.DMA((4,))] * 2,
         name="finish",
-    )(g, w)
+    )(*arrays)
 
 
 def per_device(inputs, queries, keys, values, attn_out, grad_out, lse_shift, labels, layout):
-    g, w = solve(labels, layout, lse_shift, queries, keys, values, attn_out, grad_out, inputs)
-    return finish(g, w)
+    grads = solve(labels, layout, lse_shift, queries, keys, values, attn_out, grad_out, inputs)
+    return finish(*grads)
 
 
 def solution(mesh):

time: 75.5 us -> 73.3 us (0.971)
  Pallas kernels: 74.7 us -> 72.5 us
    pallas_call x2, Pallas kernels: 74.7 us -> 72.5 us  [the longest x1 70.5 us: solve(): pl.pallas_call(solve_kernel, out_shape=(*(jax.ShapeDtypeStruct((1, TOK, H...]
where the time goes in v4:
time: 73.3 us; the launch traced here: 73.1 us
  Pallas kernels  72.5 us (99%)
    pallas_call x1, Pallas kernels, solve(): pl.pallas_call(solve_kernel, out_shape=(*(jax.ShapeDtypeStruct((1, TOK, H...  70.5 us
    pallas_call x1, Pallas kernels, finish(): pl.pallas_call(finish_kernel, out_shape=tuple((jax.ShapeDtypeStruct(a.sha...  1.96 us

profile of v4, /device:TPU:0, one launch (start us, length us, event | category | flops | bytes accessed | tf_op | source)
XLA Modules:
  0.0 73.1 jit_solution(11456797857985441073)
XLA Ops:
  0.6 70.5 %solve.1 = (bf16[1,256,512]{2,1,0:T(8,128)(2,1)}, bf16[1,256,512]{2,1,0:T(8,128)(2,1)}, bf16[1,256,512]{2,1,0:T(8,128)(2,1)}, f32[32,1536]{1,0:T(8,128)}) custom-call(s32[1,16]{1,0:T(1,128)} %labels_hbm.1, s32[1,16]{1,0:T(1,128)} %layout_hbm.1, f32[1,4,256]{2,1,0:T(4,128)} %lse_hbm.1, bf16[1,256,4096]{2,1,0:T(8,128)(2,1)} %x_hbm.1, bf16[1,256,512]{2,1,0:T(8,128)(2,1)} %o.1, ...), custom_call_target="tpu_custom_call" | custom-call | tf_op jit(solution)/shard_map/solve/pallas_call | solution.py:473
  71.2 2.0 %finish.1 = (bf16[1,256,512]{2,1,0:T(8,128)(2,1)}, bf16[1,256,512]{2,1,0:T(8,128)(2,1)}, bf16[1,256,512]{2,1,0:T(8,128)(2,1)}, f32[32,1536]{1,0:T(8,128)}) custom-call(bf16[1,256,512]{2,1,0:T(8,128)(2,1)} %get-tuple-element.8.refs_0_, bf16[1,256,512]{2,1,0:T(8,128)(2,1)} %get-tuple-element.9.refs_1_, bf16[1,256,512]{2,1,0:T(8,128)(2,1)} %get-tuple-element.10.refs_2_, ...), custom_call_target="tpu_custom_call" | custom-call | tf_op jit(solution)/shard_map/finish/pallas_call | solution.py:502

commit v5 on v4

--- a/solution.py
+++ b/solution.py
@@ -397,8 +397,6 @@
     for one, two in zip(first, second):
         one.combine()
         two.start1()
-    for one in first:
-        one.finish1()
     outs = [
         pltpu.make_async_copy(g.at[0, n, h], dst.at[0, :, h * HD : (h + 1) * HD], gout.at[n, h])
         for n, dst in enumerate((gq_out, gk_out, gv_out))
@@ -406,7 +404,8 @@
     ]
     for c in outs:
         c.start()
-    for two in second:
+    for one, two in zip(first, second):
+        one.finish1()
         two.combine()
     for one in first:
         one.finish2()

time: 73.3 us -> 73.3 us (level)
  no operation moved by 1% of the time
where the time goes in v5:
time: 73.3 us; the launch traced here: 73.1 us
  Pallas kernels  72.5 us (99%)
    pallas_call x1, Pallas kernels, solve(): pl.pallas_call(solve_kernel, out_shape=(*(jax.ShapeDtypeStruct((1, TOK, H...  70.5 us
    pallas_call x1, Pallas kernels, finish(): pl.pallas_call(finish_kernel, out_shape=tuple((jax.ShapeDtypeStruct(a.sha...  1.96 us

profile of v5, /device:TPU:0, one launch (start us, length us, event | category | flops | bytes accessed | tf_op | source)
XLA Modules:
  0.0 73.1 jit_solution(10011022352149053233)
XLA Ops:
  0.6 70.5 %solve.1 = (bf16[1,256,512]{2,1,0:T(8,128)(2,1)}, bf16[1,256,512]{2,1,0:T(8,128)(2,1)}, bf16[1,256,512]{2,1,0:T(8,128)(2,1)}, f32[32,1536]{1,0:T(8,128)}) custom-call(s32[1,16]{1,0:T(1,128)} %labels_hbm.1, s32[1,16]{1,0:T(1,128)} %layout_hbm.1, f32[1,4,256]{2,1,0:T(4,128)} %lse_hbm.1, bf16[1,256,4096]{2,1,0:T(8,128)(2,1)} %x_hbm.1, bf16[1,256,512]{2,1,0:T(8,128)(2,1)} %o.1, ...), custom_call_target="tpu_custom_call" | custom-call | tf_op jit(solution)/shard_map/solve/pallas_call | solution.py:472
  71.2 2.0 %finish.1 = (bf16[1,256,512]{2,1,0:T(8,128)(2,1)}, bf16[1,256,512]{2,1,0:T(8,128)(2,1)}, bf16[1,256,512]{2,1,0:T(8,128)(2,1)}, f32[32,1536]{1,0:T(8,128)}) custom-call(bf16[1,256,512]{2,1,0:T(8,128)(2,1)} %get-tuple-element.8.refs_0_, bf16[1,256,512]{2,1,0:T(8,128)(2,1)} %get-tuple-element.9.refs_1_, bf16[1,256,512]{2,1,0:T(8,128)(2,1)} %get-tuple-element.10.refs_2_, ...), custom_call_target="tpu_custom_call" | custom-call | tf_op jit(solution)/shard_map/finish/pallas_call | solution.py:501
